TPU v7x, 32 devices: a whole 2x2x4 slice. The times are simulated.
32 devices in a mesh: batch: 8 (over z, y), head: 4 (over x, core).
Axes of the slice: x: 2, y: 2, z: 4, core: 2. Of those that a mesh axis runs over, the one named last changes fastest.
Arguments:
- tokens: bfloat16 [16384, 768], P(('batch', 'head')), may hold values from -6 to 6
- cotangent: bfloat16 [16384, 768], P(('batch', 'head')), may hold values from -6 to 6
- lengths: int32 [32], P('batch'), may hold values from 16 to 512, as said below
- labels: int32 [32], P('batch'), may hold values from 0 to 2
- w_qkv: bfloat16 [768, 2304], replicated, may hold values from -0.21875 to 0.21875
- w_out: bfloat16 [768, 768], replicated, may hold values from -0.875 to 0.875
- w_up: bfloat16 [768, 3072], replicated, may hold values from -0.21875 to 0.21875
- w_down: bfloat16 [3072, 768], replicated, may hold values from -0.109375 to 0.109375
- w_pool: bfloat16 [768, 768], replicated, may hold values from -0.21875 to 0.21875
- w_class: bfloat16 [3, 768], replicated, may hold values from -0.625 to 0.625
- biases: float32 [7, 768], replicated, may hold values from -3 to 3
- norm_gains: float32 [2, 768], replicated, may hold values from 0.25 to 1.75
- bias_up: float32 [3072], replicated, may hold values from -3 to 3
Outputs:
- out: bfloat16 [16384, 768], P(('batch', 'head'))
- grad_tokens: bfloat16 [16384, 768], P(('batch', 'head'))
- losses: float32 [32], P(('batch', 'head'))
- g_qkv: float32 [768, 2304], P(None, ('batch', 'head'))
- g_out: float32 [768, 768], P(None, ('batch', 'head'))
- g_up: float32 [768, 3072], P(None, ('batch', 'head'))
- g_down: float32 [3072, 768], P(None, ('batch', 'head'))
- g_pool: float32 [768, 768], P(None, ('batch', 'head'))
- g_class: float32 [3, 768], P(None, ('batch', 'head'))
- g_biases: float32 [6, 768], P(None, ('batch', 'head'))
- g_gains: float32 [2, 768], P(None, ('batch', 'head'))
- g_bias_up: float32 [3072], P(('batch', 'head'))
- g_pool_bias: float32 [768], P(('batch', 'head'))
Inputs may be any that keep to these rules, and one draw needn't show every extreme that they name: `lengths`: some sequence has exactly 512 and some exactly 16 positions.
All inputs are finite; a program needn't handle non-finite values.
Results may differ from a plain program's by a relative error of at most 0.014.
Values may be sent and summed in bfloat16 or wider, within the bound.
A program may use at most 192 MiB of HBM per device.

v0:
```python
import functools

import jax
import jax.numpy as jnp
from jax import lax
from jax.experimental import pallas as pl
from jax.experimental.pallas import tpu as pltpu
from jax.sharding import PartitionSpec as P

D = 768
HEADS = 12
HEAD_DIM = 64
FF = 3072
CLASSES = 3
SLOT = 512
MESH = pl.DeviceIdType.MESH
LOW = jnp.bfloat16
F32 = jnp.float32


def layer_norm(hidden, gain, shift):
    center = hidden - jnp.mean(hidden, axis=-1, keepdims=True)
    spread = jnp.mean(center * center, axis=-1, keepdims=True)
    return center * lax.rsqrt(spread + 1e-12) * gain + shift


def exact_gelu(hidden):
    return jax.nn.gelu(hidden, approximate=False)


def inner(left, right):
    return lax.dot_general(
        left, right, (((0,), (0,)), ((), ())), preferred_element_type=jnp.float32
    )


def against(left, right):
    return lax.dot_general(
        left, right, (((1,), (1,)), ((), ())), preferred_element_type=jnp.float32
    )


def exact(left, right):
    return jnp.dot(left, right, precision=lax.Precision.HIGHEST, preferred_element_type=jnp.float32)


class Place:
    def __init__(self, rest):
        batch = lax.axis_index("batch")
        head = lax.axis_index("head")
        self.rest = rest
        self.z = batch // 2
        self.y = lax.rem(batch, 2)
        self.x = head // 2
        self.c = lax.rem(head, 2)

    def device(self, z, y, x, c):
        return (z * 2 + y, x * 2 + c)

    def core_peer(self):
        return self.device(self.z, self.y, self.x, 1 - self.c)

    def x_peer(self):
        return self.device(self.z, self.y, 1 - self.x, self.c)

    def y_peer(self):
        return self.device(self.z, 1 - self.y, self.x, self.c)

    def z_at(self, offset):
        return lax.rem(self.z + offset, self.rest)

    def z_peer(self, offset):
        return self.device(self.z_at(offset), self.y, self.x, self.c)

    def barrier(self):
        sem = pltpu.get_barrier_semaphore()
        for peer in (self.core_peer(), self.x_peer(), self.y_peer()):
            pl.semaphore_signal(sem, inc=1, device_id=peer, device_id_type=MESH)
        for offset in range(1, self.rest):
            pl.semaphore_signal(sem, inc=1, device_id=self.z_peer(offset), device_id_type=MESH)
        pl.semaphore_wait(sem, 3 + self.rest - 1)


def remote(src, dst, send, recv, peer):
    return pltpu.make_async_remote_copy(
        src_ref=src, dst_ref=dst, send_sem=send, recv_sem=recv, device_id=peer, device_id_type=MESH
    )


class Reduce:
    def __init__(self, place, part, bufs, sems, x_first):
        self.place, self.part, self.x_first = place, part, x_first
        self.r1, self.r2, self.r3, self.r4 = bufs
        send, recv, zsend, zrecv = sems
        p = place
        if x_first:
            far, near, second_far, second_near = (1 - p.x, p.x, 1 - p.y, p.y)
            peers = (p.x_peer(), p.y_peer())
            src2 = self.r1.at[far]
        else:
            far, near, second_far, second_near = (1 - p.y, p.y, 1 - p.x, p.x)
            peers = (p.y_peer(), p.x_peer())
            src2 = self.r1.at[:, far]
        self.near, self.second_near = near, second_near
        self.copies = [
            remote(part.at[1 - p.c], self.r1, send.at[0], recv.at[0], p.core_peer()),
            remote(src2, self.r2, send.at[1], recv.at[1], peers[0]),
            remote(self.r2.at[second_far], self.r3, send.at[2], recv.at[2], peers[1]),
        ]
        self.last = [
            remote(self.r3.at[p.z_at(k)], self.r4.at[k - 1], zsend.at[k - 1], zrecv.at[k - 1], p.z_peer(k))
            for k in range(1, p.rest)
        ]

    def start(self):
        self.copies[0].start()

    def step1(self):
        p = self.place
        self.copies[0].wait()
        for i in range(2):
            for j in range(2):
                def add(k, carry, i=i, j=j):
                    self.r1[i, j, k] = self.r1[i, j, k] + self.part[p.c, i, j, k]
                    return carry
                lax.fori_loop(0, p.rest, add, 0)
        self.copies[1].start()

    def step2(self):
        p = self.place
        self.copies[1].wait()
        for i in range(2):
            def add(k, carry, i=i):
                own = self.r1[self.near, i, k] if self.x_first else self.r1[i, self.near, k]
                self.r2[i, k] = self.r2[i, k] + own
                return carry
            lax.fori_loop(0, p.rest, add, 0)
        self.copies[2].start()

    def step3(self):
        p = self.place
        self.copies[2].wait()

        def add(k, carry):
            self.r3[k] = self.r3[k] + self.r2[self.second_near, k]
            return carry
        lax.fori_loop(0, p.rest, add, 0)
        for copy in self.last:
            copy.start()

    def total(self):
        p = self.place
        for copy in self.last:
            copy.wait()
        result = self.r3[p.z].astype(F32)
        for k in range(1, p.rest):
            result = result + self.r4[k - 1].astype(F32)
        return result


def chunk_scratch(rest, rows, width):
    return [
        pltpu.VMEM((2, 2, rest, rows, width), LOW),
        pltpu.VMEM((2, rest, rows, width), LOW),
        pltpu.VMEM((rest, rows, width), LOW),
        pltpu.VMEM((rest - 1, rows, width), LOW),
        pltpu.SemaphoreType.DMA((3,)),
        pltpu.SemaphoreType.DMA((3,)),
        pltpu.SemaphoreType.DMA((rest - 1,)),
        pltpu.SemaphoreType.DMA((rest - 1,)),
    ]


class Small:
    def __init__(self, place, small, lead, everyone, bufs):
        got, gotz, send, recv, zsend, zrecv, gsend, grecv, gzsend, gzrecv = bufs
        p = place
        self.place, self.small, self.got, self.gotz = p, small, got, gotz
        self.lead, self.everyone = lead, everyone
        peers = (p.core_peer(), p.x_peer(), p.y_peer())
        blocks = (
            everyone.at[p.z, p.y, p.x, p.c], everyone.at[p.z, p.y, p.x], everyone.at[p.z, p.y],
        )
        self.sums = [remote(small, got.at[i], send.at[i], recv.at[i], peers[i]) for i in range(3)]
        self.sum_last = [
            remote(small, gotz.at[k - 1], zsend.at[k - 1], zrecv.at[k - 1], p.z_peer(k)) for k in range(1, p.rest)
        ]
        self.gathers = [remote(blocks[i], blocks[i], gsend.at[i], grecv.at[i], peers[i]) for i in range(3)]
        self.gather_last = [
            remote(everyone.at[p.z], everyone.at[p.z], gzsend.at[k - 1], gzrecv.at[k - 1], p.z_peer(k))
            for k in range(1, p.rest)
        ]

    def gather_start(self):
        p = self.place
        self.everyone[p.z, p.y, p.x, p.c] = self.lead[...]
        self.gathers[0].start()

    def gather_step(self, i):
        self.gathers[i].wait()
        if i < 2:
            self.gathers[i + 1].start()
        else:
            for copy in self.gather_last:
                copy.start()

    def gather_end(self):
        for copy in self.gather_last:
            copy.wait()

    def sum_start(self):
        self.sums[0].start()

    def sum_step(self, i):
        self.sums[i].wait()
        self.small[...] = self.small[...] + self.got[i]
        if i < 2:
            self.sums[i + 1].start()
        else:
            for copy in self.sum_last:
                copy.start()

    def sum_end(self):
        for copy in self.sum_last:
            copy.wait()
        total = self.small[...]
        for k in range(1, self.place.rest):
            total = total + self.gotz[k - 1]
        return total


def small_scratch(rest):
    return [
        pltpu.VMEM((3, 16, D), F32),
        pltpu.VMEM((rest - 1, 16, D), F32),
    ] + [pltpu.SemaphoreType.DMA((3,)), pltpu.SemaphoreType.DMA((3,)),
         pltpu.SemaphoreType.DMA((rest - 1,)), pltpu.SemaphoreType.DMA((rest - 1,))] * 2


def reduce_kernel(rest, n_chunks, *refs):
    parts = refs[:n_chunks]
    small_in, lead = refs[n_chunks : n_chunks + 2]
    outs = refs[n_chunks + 2 : 2 * n_chunks + 2]
    small_out, everyone = refs[2 * n_chunks + 2 : 2 * n_chunks + 4]
    scratch = refs[2 * n_chunks + 4 :]
    place = Place(rest)
    chunks = []
    for i in range(n_chunks):
        own = scratch[8 * i : 8 * i + 8]
        chunks.append(Reduce(place, parts[i], own[:4], own[4:], i % 2 == 0))
    rest_scratch = scratch[8 * n_chunks :]
    small = Small(place, rest_scratch[0], lead, everyone, rest_scratch[1:])
    rest_scratch[0][...] = small_in[...]
    place.barrier()
    small.gather_start()
    small.sum_start()
    steps = [[c.step1, c.step2, c.step3] for c in chunks]
    for chunk in chunks:
        chunk.start()
    for i in range(3):
        small.gather_step(i)
        small.sum_step(i)
    for phase in range(n_chunks + 4):
        for i in range(n_chunks):
            k = phase - i
            if i % 2 == 1:
                k = phase - i + 1
            if 0 <= k < 3:
                steps[i][k]()
            if k == 3:
                outs[i][...] = chunks[i].total()
    small.gather_end()
    small_out[...] = small.sum_end()


def reduce_gradients(rest, parts, small, lead):
    vmem = pl.BlockSpec(memory_space=pltpu.VMEM)
    scratch = []
    for part in parts:
        scratch += chunk_scratch(rest, *part.shape[4:])
    scratch += [pltpu.VMEM((16, D), F32)] + small_scratch(rest)
    outs = [jax.ShapeDtypeStruct(part.shape[4:], F32) for part in parts]
    outs += [
        jax.ShapeDtypeStruct((16, D), F32),
        jax.ShapeDtypeStruct((rest, 2, 2, 2, 2, D), F32),
    ]
    return pl.pallas_call(
        functools.partial(reduce_kernel, rest, len(parts)),
        out_shape=tuple(outs),
        in_specs=[vmem] * (len(parts) + 2),
        out_specs=tuple([vmem] * len(outs)),
        scratch_shapes=scratch,
        compiler_params=pltpu.CompilerParams(
            collective_id=0, has_side_effects=True, vmem_limit_bytes=60 << 20
        ),
    )(*parts, small, lead)


def owner_blocks(grad_t, rest, width):
    rows = grad_t.shape[0] // (8 * rest)
    view = grad_t.astype(LOW).reshape(rest, 2, 2, 2, rows, width)
    return view.transpose(3, 2, 1, 0, 4, 5)


def attention(packed, length):
    heads = packed.reshape(SLOT, 3, HEADS, HEAD_DIM)
    queries, keys_all, values = heads[:, 0], heads[:, 1], heads[:, 2]
    scores = jnp.einsum("qhd,khd->hqk", queries, keys_all, preferred_element_type=F32) * HEAD_DIM ** (-0.5)
    scores = jnp.where((jnp.arange(SLOT) < length)[None, None, :], scores, -1e30)
    row_max = jnp.max(scores, axis=-1, keepdims=True)
    weights = jnp.exp(scores - row_max)
    weights = weights / jnp.sum(weights, axis=-1, keepdims=True)
    low = weights.astype(LOW)
    context = jnp.einsum("hqk,khd->qhd", low, values, preferred_element_type=F32)
    return context.astype(LOW).reshape(SLOT, D), low


def attention_back(packed, low, d_context):
    heads = packed.reshape(SLOT, 3, HEADS, HEAD_DIM)
    queries, keys_all, values = heads[:, 0], heads[:, 1], heads[:, 2]
    d_heads = d_context.reshape(SLOT, HEADS, HEAD_DIM)
    weights = low.astype(F32)
    d_weights = jnp.einsum("qhd,khd->hqk", d_heads, values, preferred_element_type=F32)
    d_values = jnp.einsum("hqk,qhd->khd", low, d_heads, preferred_element_type=F32)
    row_dot = jnp.sum(weights * d_weights, axis=-1, keepdims=True)
    d_scores = (weights * (d_weights - row_dot)).astype(LOW)
    scale = HEAD_DIM ** (-0.5)
    d_queries = jnp.einsum("hqk,khd->qhd", d_scores, keys_all, preferred_element_type=F32) * scale
    d_keys = jnp.einsum("hqk,qhd->khd", d_scores, queries, preferred_element_type=F32) * scale
    return jnp.stack([d_queries, d_keys, d_values], axis=1).astype(LOW).reshape(SLOT, 3 * D)


def nn(left, right):
    return jnp.dot(left, right, preferred_element_type=F32)


def aligned(index, step):
    return pl.ds(pl.multiple_of(index * step, step), step)


def column_sum(ones, array):
    return nn(ones, array)[0:1]


def normalized(hidden):
    center = hidden - jnp.mean(hidden, axis=-1, keepdims=True)
    spread = jnp.mean(center * center, axis=-1, keepdims=True)
    scale = lax.rsqrt(spread + 1e-12)
    return center * scale, scale


def normalized_back(normed, scale, d_normed):
    first = jnp.mean(d_normed, axis=-1, keepdims=True)
    second = jnp.mean(d_normed * normed, axis=-1, keepdims=True)
    return scale * (d_normed - first - normed * second)


class Staged:
    def __init__(self, place, order, part, bufs, send, recv, zsend, zrecv):
        p = self.place = place
        self.part, self.bufs = part, bufs
        sizes = {"x": 2, "y": 2, "z": p.rest}
        mine = {"x": p.x, "y": p.y, "z": p.z}
        peers = {"x": p.x_peer, "y": p.y_peer}
        self.count = 4 * p.rest
        self.stages = [[remote(part.at[pl.ds((1 - p.c) * self.count, self.count)], bufs[0], send.at[0], recv.at[0], p.core_peer())]]
        self.own = [lambda: part[pl.ds(p.c * self.count, self.count)]]
        self.got = [(bufs[0], 1, self.count)]
        blocks = self.count
        held = bufs[0]
        for i, axis in enumerate(order):
            blocks = blocks // sizes[axis]
            buf = bufs[i + 1]
            at = mine[axis]
            if axis == "z":
                copies = [
                    remote(
                        held.at[pl.ds(p.z_at(k) * blocks, blocks)], buf.at[pl.ds((k - 1) * blocks, blocks)],
                        zsend.at[k - 1], zrecv.at[k - 1], p.z_peer(k),
                    )
                    for k in range(1, p.rest)
                ]
                self.got.append((buf, p.rest - 1, blocks))
            else:
                copies = [
                    remote(held.at[pl.ds((1 - at) * blocks, blocks)], buf, send.at[i + 1], recv.at[i + 1], peers[axis]())
                ]
                self.got.append((buf, 1, blocks))
            self.stages.append(copies)
            self.own.append(lambda held=held, at=at, blocks=blocks: held[pl.ds(at * blocks, blocks)])
            held = buf

    def start(self, i):
        for copy in self.stages[i]:
            copy.start()

    def take(self, i):
        for copy in self.stages[i]:
            copy.wait()
        buf, pieces, blocks = self.got[i]
        if pieces == 1:
            buf[...] = buf[...] + self.own[i]()
        else:
            buf[0:blocks] = self.sum(i).astype(LOW)

    def sum(self, i):
        buf, pieces, blocks = self.got[i]
        total = self.own[i]().astype(F32)
        for k in range(pieces):
            total = total + buf[k * blocks : (k + 1) * blocks].astype(F32)
        return total

    def step(self, i):
        self.take(i)
        self.start(i + 1)

    def finish(self):
        i = len(self.stages) - 1
        for copy in self.stages[i]:
            copy.wait()
        return self.sum(i)[0]


def block_index(order, rest, z, y, x, c):
    sizes = {"x": 2, "y": 2, "z": rest}
    at = {"x": x, "y": y, "z": z}
    index = c
    for axis in order:
        index = index * sizes[axis] + at[axis]
    return index


def owners(rest):
    return [(z, y, x, c) for z in range(rest) for y in range(2) for x in range(2) for c in range(2)]


def staged_scratch(rest, order, rows, width):
    sizes = {"x": 2, "y": 2, "z": rest}
    blocks = 4 * rest
    bufs = [pltpu.VMEM((blocks, rows, width), LOW)]
    for axis in order:
        blocks = blocks // sizes[axis]
        copies = rest - 1 if axis == "z" else 1
        bufs.append(pltpu.VMEM((copies * blocks, rows, width), LOW))
    return bufs


ORDERS = ("xyz", "yxz", "xyz", "yxz", "xzy", "yzx")
N_IN = 13
N_OUT = 11


def layer_kernel(rest, *refs):
    (lengths, labels, biases, gains, bias_up, w_class, tokens_h, cot_h, wqkv_h, wout_h, wup_h, wdown_h, wpool_h) = refs[:N_IN]
    out_h, gtok_h, *sums = refs[N_IN : N_IN + 8]
    small_out, everyone, loss_out = refs[N_IN + 8 : N_IN + N_OUT]
    scratch = list(refs[N_IN + N_OUT :])
    (
        tokens, w_qkv, w_out, w_up, shared, packed, weights, inverse, context, normed_one, norm_low,
        activated, slope, d_hidden, d_low, d_packed, part_down, scale_one, small, lead, in_sem, out_sem,
    ) = scratch[:22]
    cot = d_low
    d_context = norm_low
    wide = SLOT
    pool_wide = d_packed.at[0:D]
    pool_rest = d_packed.at[D : 2 * D, 0 : D - wide]
    out_wide = d_packed.at[2 * D : 2 * D + SLOT]
    out_rest = d_packed.at[D : D + SLOT, wide // 2 : wide // 2 + D - wide]
    place = Place(rest)
    small_bufs = scratch[22:32]
    chunk_bufs = scratch[32:]
    head_rank = lax.axis_index("head")
    length = lengths[head_rank]
    label = labels[head_rank]
    loads = [
        pltpu.make_async_copy(src, dst, in_sem.at[i])
        for i, (src, dst) in enumerate(
            [(tokens_h, tokens), (wqkv_h, w_qkv), (wout_h, w_out), (wup_h, w_up),
             (wdown_h, shared), (cot_h, cot), (wpool_h.at[:, 0:wide], pool_wide), (wpool_h.at[:, wide:D], pool_rest)]
        )
    ]
    for load in loads:
        load.start()
    sem = pltpu.get_barrier_semaphore()
    for peer in (place.core_peer(), place.x_peer(), place.y_peer()):
        pl.semaphore_signal(sem, inc=1, device_id=peer, device_id_type=MESH)
    for offset in range(1, rest):
        pl.semaphore_signal(sem, inc=1, device_id=place.z_peer(offset), device_id_type=MESH)

    half = FF // 2
    per = 8 * rest
    chunk_parts = [part_down.at[0:per], part_down.at[per : 2 * per]]
    rows_up = FF // per // 2
    shared_blocks = shared.reshape(2 * per, rows_up, D)
    chunk_parts += [shared_blocks.at[0:per], shared_blocks.at[per : 2 * per]] * 2
    chunks = []
    for i in range(6):
        own = chunk_bufs[8 * i : 8 * i + 8]
        chunks.append(Staged(place, ORDERS[i], chunk_parts[i], own[:4], *own[4:]))
    tiny = Small(place, small, lead, everyone, small_bufs)

    loads[0].wait()
    loads[1].wait()
    ones = jnp.ones((8, SLOT), LOW)
    for part in range(3):
        columns = slice(part * D, part * D + D)
        result = nn(tokens[...], w_qkv[:, columns])
        if part == 0:
            result = (result + biases[0:1]).astype(LOW) * jnp.asarray(HEAD_DIM ** (-0.5), LOW)
        elif part == 2:
            result = (result + biases[1:2]).astype(LOW)
        else:
            result = result.astype(LOW)
        packed[:, columns] = result

    key_live = lax.broadcasted_iota(jnp.int32, (SLOT, 1), 0) < length
    lane = lax.broadcasted_iota(jnp.int32, (1, 2 * HEAD_DIM), 1)
    lane_of = [lane < HEAD_DIM, lane >= HEAD_DIM]

    def attend(pair, carry):
        at = pl.multiple_of(pair * 2 * HEAD_DIM, 2 * HEAD_DIM)
        queries = packed[:, pl.ds(at, 2 * HEAD_DIM)]
        keys_all = packed[:, pl.ds(at + D, 2 * HEAD_DIM)]
        values_t = packed[:, pl.ds(at + 2 * D, 2 * HEAD_DIM)].T
        got = []
        for k in range(2):
            own_keys = jnp.where(lane_of[k], keys_all, jnp.zeros_like(keys_all))
            scores = jnp.where(key_live, against(own_keys, queries), -1e30)
            powers = jnp.exp(scores - jnp.max(scores, axis=0, keepdims=True))
            inv = 1.0 / jnp.sum(powers, axis=0, keepdims=True)
            powers = powers.astype(LOW)
            weights[2 * pair + k] = powers
            inverse[pair, k : k + 1] = inv
            got.append(nn(values_t[k * HEAD_DIM : (k + 1) * HEAD_DIM], powers) * inv)
        context[:, pl.ds(at, 2 * HEAD_DIM)] = jnp.concatenate(got, axis=0).T.astype(LOW)
        return carry

    lax.fori_loop(0, HEADS // 2, attend, 0)

    blocks = [slice(0, SLOT // 2), slice(SLOT // 2, SLOT)]
    loads[2].wait()
    for rows in blocks:
        hidden = nn(context[rows], w_out[...]) + biases[2:3] + tokens[rows].astype(F32)
        normed, scale = normalized(hidden)
        normed_one[rows] = normed
        scale_one[rows] = scale
        norm_low[rows] = (normed * gains[0:1] + biases[3:4]).astype(LOW)

    loads[3].wait()

    def feed(tile, carry):
        columns = aligned(tile, D)
        hidden = nn(norm_low[...], w_up[:, columns]) + bias_up[0:1, columns]
        share = 0.5 + 0.5 * lax.erf(hidden * 0.7071067811865476)
        activated[:, columns] = (hidden * share).astype(LOW)
        slope[:, columns] = (share + hidden * (jnp.exp(-0.5 * hidden * hidden) * 0.3989422804014327)).astype(LOW)
        return carry

    lax.fori_loop(0, FF // D, feed, 0)

    w_down = shared
    for i in (4, 5, 6, 7):
        loads[i].wait()
    row = lax.broadcasted_iota(jnp.int32, (SLOT // 2, 1), 0)
    kept = []
    for k, rows in enumerate(blocks):
        hidden = nn(activated[rows], w_down[...]) + biases[4:5] + (normed_one[rows] * gains[0:1] + biases[3:4])
        normed, scale = normalized(hidden)
        result = normed * gains[1:2] + biases[5:6]
        low = result.astype(LOW)
        out_wide[rows] = low[:, 0:wide]
        out_rest[rows] = low[:, wide:D]
        d_hidden[rows] = normed
        kept.append(scale)
        if k == 0:
            leading = low[0:8]
    out_copies = [
        pltpu.make_async_copy(out_wide, out_h.at[:, 0:wide], out_sem.at[0]),
        pltpu.make_async_copy(out_rest, out_h.at[:, wide:D], out_sem.at[2]),
    ]
    for copy in out_copies:
        copy.start()

    pooled = jnp.concatenate([nn(leading, pool_wide[...]), nn(leading, pool_rest[...])], axis=1)
    pooled = jnp.tanh(pooled + biases[6:7])[0:1]
    pooled_low = pooled.astype(LOW).astype(F32)
    classes = w_class[...].astype(F32)
    logits = jnp.sum(pooled_low * classes, axis=-1, keepdims=True)
    top = jnp.max(logits, axis=0, keepdims=True)
    powers = jnp.exp(logits - top)
    total = jnp.sum(powers, axis=0, keepdims=True)
    onehot = (lax.broadcasted_iota(jnp.int32, (CLASSES, 1), 0) == label).astype(F32)
    loss_out[...] = jnp.broadcast_to(
        jnp.log(total) + top - jnp.sum(onehot * logits, axis=0, keepdims=True), loss_out.shape
    )
    d_logits = powers / total - onehot
    d_pre = jnp.sum(d_logits * classes, axis=0, keepdims=True) * (1.0 - pooled * pooled)
    high = d_pre.astype(LOW).astype(F32)
    middle = (d_pre - high).astype(LOW).astype(F32)
    low = d_pre - high - middle
    eight = lax.broadcasted_iota(jnp.int32, (8, 1), 0)
    split = jnp.where(eight == 0, high, jnp.where(eight == 1, middle, jnp.where(eight == 2, low, 0.0)))
    split = split.astype(LOW)
    d_leading = against(split[:, 0:wide], pool_wide[...]) + against(split[:, wide:D], pool_rest[...])
    d_leading = jnp.sum(d_leading, axis=0, keepdims=True)
    small[0:3] = d_logits * pooled_low
    small[15:16] = d_pre
    lead[0:1] = leading[0:1].astype(F32)
    lead[1:2] = d_pre

    shift_two = jnp.zeros((1, D), F32)
    gain_two = jnp.zeros((1, D), F32)
    for k in (1, 0):
        rows = blocks[k]
        normed, scale = d_hidden[rows], kept[k]
        d_out = jnp.where(row + k * (SLOT // 2) < length, cot[rows].astype(F32), 0.0)
        if k == 0:
            d_out = d_out + jnp.where(row == 0, d_leading, 0.0)
        shift_two = shift_two + jnp.sum(d_out, axis=0, keepdims=True)
        gain_two = gain_two + jnp.sum(d_out * normed, axis=0, keepdims=True)
        d_two = normalized_back(normed, scale, d_out * gains[1:2])
        d_hidden[rows] = d_two
        d_low[rows] = d_two.astype(LOW)
    small[8:9] = shift_two
    small[10:11] = gain_two
    small[7:8] = column_sum(ones, d_low[...])

    for copy in out_copies:
        copy.wait()
    pl.semaphore_wait(sem, 3 + rest - 1)
    tiny.gather_start()
    d_branch_t = d_low[...].T
    rows_down = D // per
    for chunk in range(2):
        for tile in range(4):
            columns = slice(tile * D // 2, (tile + 1) * D // 2)
            result = nn(d_branch_t, activated[:, chunk * half + columns.start : chunk * half + columns.stop])
            for d, owner in enumerate(owners(rest)):
                part_down[chunk * per + block_index(ORDERS[chunk], rest, *owner), :, columns] = (
                    result[d * rows_down : (d + 1) * rows_down].astype(LOW)
                )
        chunks[chunk].start(0)

    def feed_back(tile, carry):
        columns = aligned(tile, D)
        d_up = (against(d_low[...], w_down[columns]) * slope[:, columns].astype(F32)).astype(LOW)
        slope[:, columns] = d_up
        small[pl.ds(11 + tile, 1)] = column_sum(ones, d_up)
        return carry

    lax.fori_loop(0, FF // D, feed_back, 0)
    d_up = slope
    tiny.gather_step(0)
    chunks[0].step(0)
    chunks[1].step(0)

    for tile in range(FF // D):
        for columns in (slice(0, D // 2), slice(D // 2, D)):
            result = inner(d_up[:, tile * D : (tile + 1) * D], norm_low[:, columns])
            for d in range(per * D // FF):
                owner = owners(rest)[tile * (per * D // FF) + d]
                for chunk in (2, 3):
                    first = d * 2 * rows_up + (chunk - 2) * rows_up
                    shared_blocks[(chunk - 2) * per + block_index(ORDERS[chunk], rest, *owner), :, columns] = (
                        result[first : first + rows_up].astype(LOW)
                    )
    chunks[2].start(0)
    chunks[3].start(0)
    tiny.gather_step(1)

    shift_one = jnp.zeros((1, D), F32)
    gain_one = jnp.zeros((1, D), F32)
    for rows in blocks:
        d_norm = d_hidden[rows] + against(d_up[rows], w_up[...])
        normed = normed_one[rows]
        shift_one = shift_one + jnp.sum(d_norm, axis=0, keepdims=True)
        gain_one = gain_one + jnp.sum(d_norm * normed, axis=0, keepdims=True)
        d_one = normalized_back(normed, scale_one[rows], d_norm * gains[0:1])
        d_hidden[rows] = d_one
        d_low[rows] = d_one.astype(LOW)
    small[6:7] = shift_one
    small[9:10] = gain_one
    small[5:6] = column_sum(ones, d_low[...])
    chunks[2].step(0)
    chunks[3].step(0)
    tiny.gather_step(2)

    d_context[...] = against(d_low[...], w_out[...]).astype(LOW)
    result_out = inner(d_low[...], context[...])
    own_qkv = 3 * D // per
    own_out = D // per
    first_rows = rows_up - (own_qkv - rows_up)
    for d, owner in enumerate(owners(rest)):
        shared_blocks[per + block_index(ORDERS[5], rest, *owner), own_qkv - rows_up :] = (
            result_out[d * own_out : (d + 1) * own_out].astype(LOW)
        )

    def attend_back(pair, carry):
        at = pl.multiple_of(pair * 2 * HEAD_DIM, 2 * HEAD_DIM)
        queries_t = packed[:, pl.ds(at, 2 * HEAD_DIM)].T
        keys_t = packed[:, pl.ds(at + D, 2 * HEAD_DIM)].T
        values = packed[:, pl.ds(at + 2 * D, 2 * HEAD_DIM)]
        context_t = context[:, pl.ds(at, 2 * HEAD_DIM)].T
        d_context_t = d_context[:, pl.ds(at, 2 * HEAD_DIM)].T
        scaled = []
        dots = []
        for k in range(2):
            rows = slice(k * HEAD_DIM, (k + 1) * HEAD_DIM)
            own = d_context_t[rows].astype(F32) * inverse[pair, k : k + 1]
            dots.append(jnp.sum(own * context_t[rows].astype(F32), axis=0, keepdims=True))
            scaled.append(own.astype(LOW))
        both = jnp.concatenate(scaled, axis=0).T
        for k in range(2):
            rows = slice(k * HEAD_DIM, (k + 1) * HEAD_DIM)
            own_values = jnp.where(lane_of[k], values, jnp.zeros_like(values))
            powers = weights[2 * pair + k]
            d_scores = (powers.astype(F32) * (against(own_values, both) - dots[k])).astype(LOW)
            put = pl.multiple_of(at + k * HEAD_DIM, HEAD_DIM)
            d_packed[pl.ds(put, HEAD_DIM)] = (nn(keys_t[rows], d_scores) * HEAD_DIM ** (-0.5)).astype(LOW)
            d_packed[pl.ds(put + D, HEAD_DIM)] = against(queries_t[rows], d_scores).astype(LOW)
            d_packed[pl.ds(put + 2 * D, HEAD_DIM)] = against(scaled[k], powers).astype(LOW)
        return carry

    lax.fori_loop(0, 3, attend_back, 0)
    chunks[0].step(1)
    chunks[1].step(1)
    lax.fori_loop(3, HEADS // 2, attend_back, 0)

    for tile in range(rest):
        size = 8 * own_qkv
        result = nn(d_packed[tile * size : (tile + 1) * size], tokens[...])
        for d in range(8):
            owner = owners(rest)[tile * 8 + d]
            first = d * own_qkv
            shared_blocks[block_index(ORDERS[4], rest, *owner)] = result[first : first + rows_up].astype(LOW)
            shared_blocks[per + block_index(ORDERS[5], rest, *owner), : own_qkv - rows_up] = (
                result[first + rows_up : first + own_qkv].astype(LOW)
            )
    chunks[4].start(0)
    chunks[5].start(0)
    small[3:4] = against(ones, d_packed[0:D])[0:1]
    small[4:5] = against(ones, d_packed[2 * D : 3 * D])[0:1]
    tiny.sum_start()
    chunks[0].step(2)
    chunks[1].step(2)

    chunks[4].step(0)
    chunks[5].step(0)
    for k, rows in enumerate(blocks):
        d_tokens = nn(w_qkv[...], d_packed[:, rows]).T + d_hidden[rows]
        d_low[rows] = d_tokens.astype(LOW)
    token_copy = pltpu.make_async_copy(d_low, gtok_h, out_sem.at[1])
    token_copy.start()
    tiny.sum_step(0)
    chunks[2].step(1)
    chunks[3].step(1)
    sums[0][...] = chunks[0].finish()
    sums[1][...] = chunks[1].finish()
    tiny.sum_step(1)
    chunks[2].step(2)
    chunks[3].step(2)
    tiny.sum_step(2)
    chunks[4].step(1)
    chunks[5].step(1)
    sums[2][...] = chunks[2].finish()
    sums[3][...] = chunks[3].finish()
    small_out[...] = tiny.sum_end()
    tiny.gather_end()
    chunks[4].step(2)
    chunks[5].step(2)
    sums[4][...] = chunks[4].finish()
    sums[5][...] = chunks[5].finish()
    token_copy.wait()


def layer(rest, tokens, cotangent, lengths, labels, w_qkv, w_out, w_up, w_down, w_pool, w_class, biases, norm_gains, bias_up):
    per = 8 * rest
    rows_up = FF // per // 2
    rows_down = D // per
    vmem = pl.BlockSpec(memory_space=pltpu.VMEM)
    smem = pl.BlockSpec(memory_space=pltpu.SMEM)
    anywhere = pl.BlockSpec(memory_space=pl.ANY)
    dma = pltpu.SemaphoreType.DMA
    shapes = [(rows_down, FF // 2)] * 2 + [(rows_up, D)] * 4
    scratch = [
        pltpu.VMEM((SLOT, D), LOW),
        pltpu.VMEM((D, 3 * D), LOW),
        pltpu.VMEM((D, D), LOW),
        pltpu.VMEM((D, FF), LOW),
        pltpu.VMEM((FF, D), LOW),
        pltpu.VMEM((SLOT, 3 * D), LOW),
        pltpu.VMEM((HEADS, SLOT, SLOT), LOW),
        pltpu.VMEM((HEADS // 2, 2, SLOT), F32),
        pltpu.VMEM((SLOT, D), LOW),
        pltpu.VMEM((SLOT, D), F32),
        pltpu.VMEM((SLOT, D), LOW),
        pltpu.VMEM((SLOT, FF), LOW),
        pltpu.VMEM((SLOT, FF), LOW),
        pltpu.VMEM((SLOT, D), F32),
        pltpu.VMEM((SLOT, D), LOW),
        pltpu.VMEM((3 * D, SLOT), LOW),
        pltpu.VMEM((2 * per, rows_down, FF // 2), LOW),
        pltpu.VMEM((SLOT, 1), F32),
        pltpu.VMEM((16, D), F32),
        pltpu.VMEM((2, D), F32),
        dma((8,)),
        dma((3,)),
    ] + small_scratch(rest)
    for order, (rows, width) in zip(ORDERS, shapes):
        scratch += staged_scratch(rest, order, rows, width) + [dma((4,)), dma((4,)), dma((rest - 1,)), dma((rest - 1,))]
    outs = [jax.ShapeDtypeStruct((SLOT, D), LOW)] * 2 + [jax.ShapeDtypeStruct(shape, F32) for shape in shapes] + [
        jax.ShapeDtypeStruct((16, D), F32),
        jax.ShapeDtypeStruct((rest, 2, 2, 2, 2, D), F32),
        jax.ShapeDtypeStruct((1, 128), F32),
    ]
    return pl.pallas_call(
        functools.partial(layer_kernel, rest),
        out_shape=tuple(outs),
        in_specs=[smem, smem] + [vmem] * 4 + [anywhere] * 7,
        out_specs=tuple([anywhere] * 2 + [vmem] * 9),
        scratch_shapes=scratch,
        compiler_params=pltpu.CompilerParams(
            collective_id=0, has_side_effects=True, vmem_limit_bytes=61 << 20
        ),
    )(lengths, labels, biases, norm_gains, bias_up.reshape(1, FF), w_class, tokens, cotangent, w_qkv, w_out, w_up, w_down, w_pool)


def finish_kernel(rest, *refs):
    out_in, gtok_in, down1, down2, up1, up2, last1, last2, small, everyone, loss = refs[:11]
    (out, gtok, losses, g_qkv, g_out, g_up, g_down, g_pool, g_class, g_biases, g_gains, g_bias_up, g_pool_bias) = refs[11:24]
    sem = refs[24]
    copies = [pltpu.make_async_copy(out_in, out, sem.at[0]), pltpu.make_async_copy(gtok_in, gtok, sem.at[1])]
    for copy in copies:
        copy.start()
    per = 8 * rest
    rank = lax.axis_index("batch") * 4 + lax.axis_index("head")
    own = D // per
    own_qkv = 3 * own
    own_up = FF // per
    rows_up = own_up // 2
    losses[...] = loss[0:1, 0:1]
    g_down[0 : FF // 2] = down1[...].T
    g_down[FF // 2 : FF] = down2[...].T
    g_up[...] = jnp.concatenate([up1[...], up2[...]], axis=0).T
    last = jnp.concatenate([last1[...], last2[...]], axis=0).T
    g_qkv[...] = last[:, :own_qkv]
    g_out[...] = last[:, own_qkv:]

    def window(array, start, size):
        at = lax.broadcasted_iota(jnp.int32, (D, size), 0)
        want = lax.broadcasted_iota(jnp.int32, (D, size), 1)
        return exact(array, (at == want + start).astype(F32))

    picked = window(small[...], rank * own, own)
    g_class[...] = picked[0:3]
    g_biases[...] = picked[3:9]
    g_gains[...] = picked[9:11]
    g_pool_bias[...] = picked[15:16]
    flat = rank * own_up
    part = flat // D
    rows = small[11:15]
    pick = lax.broadcasted_iota(jnp.int32, (4, 1), 0) == part
    chosen = jnp.sum(jnp.where(pick, rows, 0.0), axis=0, keepdims=True)
    g_bias_up[...] = window(jnp.broadcast_to(chosen, (8, D)), flat - part * D, own_up)[0:1]
    leading = everyone[:, 0]
    d_pre = window(everyone[:, 1], rank * own, own)
    g_pool[...] = lax.dot_general(
        leading, d_pre, (((0,), (0,)), ((), ())), precision=lax.Precision.HIGHEST, preferred_element_type=F32
    )
    for copy in copies:
        copy.wait()


def finish(rest, results):
    per = 8 * rest
    own = D // per
    vmem = pl.BlockSpec(memory_space=pltpu.VMEM)
    anywhere = pl.BlockSpec(memory_space=pl.ANY)
    shape = lambda *s: jax.ShapeDtypeStruct(s, F32)
    results = list(results)
    results[9] = results[9].reshape(per, 2, D)
    outs = [jax.ShapeDtypeStruct((SLOT, D), LOW)] * 2 + [
        shape(1, 1), shape(D, 3 * own), shape(D, own), shape(D, 4 * own), shape(FF, own), shape(D, own),
        shape(3, own), shape(6, own), shape(2, own), shape(1, 4 * own), shape(1, own),
    ]
    out = list(pl.pallas_call(
        functools.partial(finish_kernel, rest),
        out_shape=tuple(outs),
        in_specs=[anywhere] * 2 + [vmem] * 9,
        out_specs=tuple([anywhere] * 2 + [vmem] * 11),
        scratch_shapes=[pltpu.SemaphoreType.DMA((2,))],
        compiler_params=pltpu.CompilerParams(vmem_limit_bytes=32 << 20),
    )(*results))
    for i in (2, 11, 12):
        out[i] = out[i].reshape(-1)
    return tuple(out)


def per_device(
    tokens,
    cotangent,
    lengths,
    labels,
    w_qkv,
    w_out,
    w_up,
    w_down,
    w_pool,
    w_class,
    biases,
    norm_gains,
    bias_up,
):
    rest = lax.axis_size("batch") // 2
    if D // (8 * rest) % 8 == 0:
        return finish(rest, layer(
            rest, tokens, cotangent, lengths, labels, w_qkv, w_out, w_up, w_down, w_pool, w_class, biases, norm_gains,
            bias_up,
        ))
    head_rank = lax.axis_index("head")
    rank = lax.axis_index("batch") * 4 + head_rank
    length = lax.dynamic_index_in_dim(lengths, head_rank, keepdims=False)
    label = lax.dynamic_index_in_dim(labels, head_rank, keepdims=False)
    slot_live = (jnp.arange(SLOT) < length).astype(F32)
    zeros_key = jnp.zeros((D,), F32)
    packed = jnp.dot(tokens, w_qkv, preferred_element_type=F32) + jnp.concatenate(
        [biases[0], zeros_key, biases[1]]
    )
    packed = packed.astype(LOW)
    context, probs = attention(packed, length)
    attn = jnp.dot(context, w_out, preferred_element_type=F32) + biases[2]
    first_sum = tokens.astype(F32) + attn
    norm_one, first_pull = jax.vjp(layer_norm, first_sum, norm_gains[0], biases[3])
    norm_low = norm_one.astype(LOW)
    hidden_up = jnp.dot(norm_low, w_up, preferred_element_type=F32) + bias_up
    activated_full, gelu_pull = jax.vjp(exact_gelu, hidden_up)
    activated = activated_full.astype(LOW)
    branch = jnp.dot(activated, w_down, preferred_element_type=F32) + biases[4]
    out_full, second_pull = jax.vjp(layer_norm, norm_one + branch, norm_gains[1], biases[5])
    leading = out_full[:1].astype(LOW)
    pooled = jnp.tanh(jnp.dot(leading, w_pool, preferred_element_type=F32) + biases[6])
    pooled_low = pooled.astype(LOW)
    logits = against(pooled_low, w_class)
    onehot = (jnp.arange(CLASSES)[None, :] == label).astype(F32)
    losses = jax.nn.logsumexp(logits, axis=-1) - jnp.sum(onehot * logits, axis=-1)
    d_logits = jax.nn.softmax(logits, axis=-1) - onehot
    g_class = exact(d_logits.T, pooled_low.astype(F32))
    d_pre = exact(d_logits, w_class.astype(F32)) * (1.0 - pooled * pooled)
    d_leading = exact(d_pre, w_pool.astype(F32).T)
    d_out = cotangent.astype(F32) * slot_live[:, None]
    d_out = d_out.at[0].add(d_leading[0])
    d_h2, g_gain_two, g_shift_two = second_pull(d_out)
    d_branch = d_h2.astype(LOW)
    g_bias_down = jnp.sum(d_branch.astype(F32), axis=0)
    g_down_t = inner(d_branch, activated)
    d_activated = against(d_branch, w_down)
    d_up = gelu_pull(d_activated)[0].astype(LOW)
    g_bias_up = jnp.sum(d_up.astype(F32), axis=0)
    g_up_t = inner(d_up, norm_low)
    d_norm_one = d_h2 + against(d_up, w_up)
    d_h1, g_gain_one, g_shift_one = first_pull(d_norm_one)
    d_attn = d_h1.astype(LOW)
    g_bias_out = jnp.sum(d_attn.astype(F32), axis=0)
    g_out_t = inner(d_attn, context)
    d_context = against(d_attn, w_out).astype(LOW)
    d_packed = attention_back(packed, probs, d_context)
    g_qkv_t = inner(d_packed, tokens)
    column_sums = jnp.sum(d_packed.astype(F32), axis=0)
    grad_tokens = (d_h1 + against(d_packed, w_qkv)).astype(LOW)
    small = jnp.concatenate(
        [
            g_class,
            jnp.stack([column_sums[:D], column_sums[2 * D :], g_bias_out, g_shift_one, g_bias_down, g_shift_two]),
            jnp.stack([g_gain_one, g_gain_two]),
            g_bias_up.reshape(FF // D, D),
            d_pre,
        ]
    )
    lead = jnp.concatenate([leading.astype(F32), d_pre])
    down = owner_blocks(g_down_t, rest, FF)
    up = owner_blocks(g_up_t, rest, D)
    last = jnp.concatenate([owner_blocks(g_qkv_t, rest, D), owner_blocks(g_out_t, rest, D)], axis=4)
    half = up.shape[4] // 2
    parts = [
        down[..., : FF // 2], down[..., FF // 2 :],
        up[..., :half, :], up[..., half:, :],
        last[..., :half, :], last[..., half:, :],
    ]
    *sums, small, everyone = reduce_gradients(rest, parts, small, lead)
    g_down = jnp.concatenate(sums[0:2], axis=1).T
    g_up = jnp.concatenate(sums[2:4], axis=0).T
    g_last = jnp.concatenate(sums[4:6], axis=0).T
    own_qkv = 3 * D // (8 * rest)
    own = D // (8 * rest)
    everyone = everyone.reshape(8 * rest, 2, D)
    window = lax.dynamic_slice_in_dim(small, rank * own, own, axis=1)
    pre_window = lax.dynamic_slice_in_dim(everyone[:, 1], rank * own, own, axis=1)
    g_pool = lax.dot_general(
        everyone[:, 0], pre_window, (((0,), (0,)), ((), ())),
        precision=lax.Precision.HIGHEST, preferred_element_type=F32,
    )
    own_up = FF // (8 * rest)
    g_bias_up = lax.dynamic_slice_in_dim(small[11:15].reshape(FF), rank * own_up, own_up)
    return (
        out_full.astype(LOW),
        grad_tokens,
        losses,
        g_last[:, :own_qkv],
        g_last[:, own_qkv:],
        g_up,
        g_down,
        g_pool,
        window[:3],
        window[3:9],
        window[9:11],
        g_bias_up,
        window[15],
    )


def solution(mesh):
    return jax.shard_map(
        per_device,
        mesh=mesh,
        in_specs=(
            P(("batch", "head"), None),
            P(("batch", "head"), None),
            P("batch"),
            P("batch"),
            P(),
            P(),
            P(),
            P(),
            P(),
            P(),
            P(),
            P(),
            P(),
        ),
        out_specs=(
            P(("batch", "head"), None),
            P(("batch", "head"), None),
            P(("batch", "head")),
            P(None, ("batch", "head")),
            P(None, ("batch", "head")),
            P(None, ("batch", "head")),
            P(None, ("batch", "head")),
            P(None, ("batch", "head")),
            P(None, ("batch", "head")),
            P(None, ("batch", "head")),
            P(None, ("batch", "head")),
            P(("batch", "head")),
            P(("batch", "head")),
        ),
        check_vma=False,
    )
```

profile of v0, /device:TPU:0, one launch (start us, length us, event | category | flops | bytes accessed | tf_op | source)
XLA Modules:
  0.0 153.7 jit_solution(4536267825747983507)
XLA Ops:
  0.6 136.3 %shard_map.228 = (bf16[512,768]{1,0:T(8,128)(2,1)}, bf16[512,768]{1,0:T(8,128)(2,1)}, f32[24,1536]{1,0:T(8,128)}, f32[24,1536]{1,0:T(8,128)}, f32[48,768]{1,0:T(...) custom-call(s32[4]{0:T(128)} %refs_0_.1, ...), custom_call_target="tpu_custom_call" | custom-call | tf_op jit(solution)/shard_map/pallas_call | solution.py:816
  137.0 0.0 copy-start
  137.0 1.1 copy-done
  138.1 0.0 copy-start.1
  138.1 1.1 copy-done.1
  139.2 0.0 copy-start.2
  139.2 0.9 copy-done.2
  140.2 0.0 copy-start.3
  140.2 0.9 copy-done.3
  141.1 0.0 copy-start.4
  141.1 0.9 copy-done.4
  142.0 0.0 copy-start.5
  142.0 0.9 copy-done.5
  142.9 0.0 copy-start.6
  142.9 0.9 copy-done.6
  143.8 0.0 copy-start.7
  143.8 0.9 copy-done.7
  144.7 0.0 copy-start.8
  144.7 0.9 copy-done.8
  145.6 0.0 copy-start.9
  145.6 0.8 copy-done.9
  146.4 0.0 copy-start.10
  146.4 0.7 copy-done.10
  147.1 2.2 %shard_map.229 = (bf16[512,768]{1,0:T(8,128)(2,1)}, bf16[512,768]{1,0:T(8,128)(2,1)}, f32[1,1]{1,0:T(1,128)}, f32[768,72]{1,0:T(8,128)S(1)}, f32[768,24]{1,0:T(8...) custom-call(bf16[512,768]{1,0:T(8,128)(2,1)S(1)} %copy-done, ...), custom_call_target="tpu_custom_call" | custom-call | tf_op jit(solution)/shard_map/pallas_call | solution.py:886
  149.3 0.8 copy.27
  150.1 0.8 copy.30
  150.8 0.8 copy.26
  151.7 0.9 copy.28
  152.5 1.2 copy.29
Async XLA Ops:
  137.0 1.1 copy-start
  138.1 1.1 copy-start.1
  139.2 0.9 copy-start.2
  140.2 0.9 copy-start.3
  141.1 0.9 copy-start.4
  142.0 0.9 copy-start.5
  142.9 0.9 copy-start.6
  143.8 0.9 copy-start.7
  144.7 0.9 copy-start.8
  145.6 0.8 copy-start.9
  146.4 0.7 copy-start.10
where the time goes:
time: 154 us
  Pallas kernels  138 us (90%)
  local copies, waits for them, and re-layouts  14.5 us (9%)
    pallas_call x1, Pallas kernels, layer(): pl.pallas_call(functools.partial(layer_kernel, rest), out_shape=tuple(out...  136 us
    unnamed x27, local copies, waits for them, and re-layouts  14.5 us

commit v1 on v0

--- a/solution.py
+++ b/solution.py
@@ -355,70 +355,139 @@
     return scale * (d_normed - first - normed * second)
 
 
-class Staged:
-    def __init__(self, place, order, part, bufs, send, recv, zsend, zrecv):
+class Unit:
+    def __init__(self, place, order, part, bufs, send, recv, put):
         p = self.place = place
-        self.part, self.bufs = part, bufs
-        sizes = {"x": 2, "y": 2, "z": p.rest}
-        mine = {"x": p.x, "y": p.y, "z": p.z}
-        peers = {"x": p.x_peer, "y": p.y_peer}
-        self.count = 4 * p.rest
-        self.stages = [[remote(part.at[pl.ds((1 - p.c) * self.count, self.count)], bufs[0], send.at[0], recv.at[0], p.core_peer())]]
-        self.own = [lambda: part[pl.ds(p.c * self.count, self.count)]]
-        self.got = [(bufs[0], 1, self.count)]
-        blocks = self.count
-        held = bufs[0]
+        self.put = put
+        self.at = 0
+        self.legs = []
+        bufs = list(bufs)
+        count = part.shape[0] // 2
+        held = bufs.pop(0)
+        copy = remote(part.at[pl.ds((1 - p.c) * count, count)], held, send.at[0], recv.at[0], p.core_peer())
+        self.legs.append((copy.start, self.pair_end(copy, held, part, p.c * count, count, False)))
+        base = 0
+        slot = 1
         for i, axis in enumerate(order):
-            blocks = blocks // sizes[axis]
-            buf = bufs[i + 1]
-            at = mine[axis]
+            last = i == len(order) - 1
             if axis == "z":
-                copies = [
-                    remote(
-                        held.at[pl.ds(p.z_at(k) * blocks, blocks)], buf.at[pl.ds((k - 1) * blocks, blocks)],
-                        zsend.at[k - 1], zrecv.at[k - 1], p.z_peer(k),
-                    )
-                    for k in range(1, p.rest)
-                ]
-                self.got.append((buf, p.rest - 1, blocks))
+                count = count // 4
+                self.line(held, base, count, bufs.pop(0), bufs.pop(0), send, recv, slot, last)
+                base = base + p.z * count
+                slot += 3
             else:
-                copies = [
-                    remote(held.at[pl.ds((1 - at) * blocks, blocks)], buf, send.at[i + 1], recv.at[i + 1], peers[axis]())
-                ]
-                self.got.append((buf, 1, blocks))
-            self.stages.append(copies)
-            self.own.append(lambda held=held, at=at, blocks=blocks: held[pl.ds(at * blocks, blocks)])
-            held = buf
-
-    def start(self, i):
-        for copy in self.stages[i]:
-            copy.start()
-
-    def take(self, i):
-        for copy in self.stages[i]:
+                count = count // 2
+                mine, peer = (p.x, p.x_peer()) if axis == "x" else (p.y, p.y_peer())
+                got = bufs.pop(0)
+                copy = remote(held.at[pl.ds(base + (1 - mine) * count, count)], got, send.at[slot], recv.at[slot], peer)
+                self.legs.append((copy.start, self.pair_end(copy, got, held, base + mine * count, count, last)))
+                held, base = got, 0
+                slot += 1
+
+    def pair_end(self, copy, got, own, start, count, last):
+        def end():
             copy.wait()
-        buf, pieces, blocks = self.got[i]
-        if pieces == 1:
-            buf[...] = buf[...] + self.own[i]()
-        else:
-            buf[0:blocks] = self.sum(i).astype(LOW)
-
-    def sum(self, i):
-        buf, pieces, blocks = self.got[i]
-        total = self.own[i]().astype(F32)
-        for k in range(pieces):
-            total = total + buf[k * blocks : (k + 1) * blocks].astype(F32)
-        return total
-
-    def step(self, i):
-        self.take(i)
-        self.start(i + 1)
-
-    def finish(self):
-        i = len(self.stages) - 1
-        for copy in self.stages[i]:
-            copy.wait()
-        return self.sum(i)[0]
+            if last:
+                self.put(got[0].astype(F32) + own[start].astype(F32))
+            else:
+                got[...] = got[...] + own[pl.ds(start, count)]
+        return end
+
+    def line(self, held, base, n, wide, single, send, recv, slot, last):
+        p = self.place
+        z = p.z
+        outer = jnp.logical_or(z == 0, z == 3)
+        inner = jnp.logical_not(outer)
+        low = z < 2
+        near = jnp.where(low, 1 - z, 5 - z)
+        far = jnp.where(low, z + 2, z - 2)
+        middle = 3 - z
+
+        def at(block, count=n):
+            return held.at[pl.ds(base + block * n, count)]
+
+        def device(block):
+            return p.device(block, p.y, p.x, p.c)
+
+        outward = remote(at(jnp.where(z == 0, 1, 0), 3 * n), wide, send.at[slot], recv.at[slot], device(near))
+        back = remote(at(near), wide.at[0:n], send.at[slot], recv.at[slot], device(near))
+        across = remote(at(middle), single, send.at[slot + 1], recv.at[slot + 1], device(middle))
+        beyond = remote(at(far), wide.at[n : 2 * n], send.at[slot + 2], recv.at[slot + 2], device(far))
+
+        def begin_first():
+            @pl.when(outer)
+            def _():
+                outward.start()
+
+            @pl.when(inner)
+            def _():
+                back.start()
+
+        def end_first():
+            @pl.when(outer)
+            def _():
+                outward.wait_send()
+                back.wait_recv()
+
+            @pl.when(inner)
+            def _():
+                back.wait_send()
+                outward.wait_recv()
+                start = base + jnp.where(z == 1, n, 0)
+                held[pl.ds(start, 3 * n)] = held[pl.ds(start, 3 * n)] + wide[...]
+
+        def begin_second():
+            @pl.when(inner)
+            def _():
+                across.start()
+                beyond.start()
+
+        def end_second():
+            @pl.when(outer)
+            def _():
+                beyond.wait_recv()
+                total = held[pl.ds(base + z * n, n)].astype(F32) + wide[0:n].astype(F32) + wide[n : 2 * n].astype(F32)
+                if last:
+                    self.put(total[0])
+                else:
+                    held[pl.ds(base + z * n, n)] = total.astype(LOW)
+
+            @pl.when(inner)
+            def _():
+                across.wait()
+                beyond.wait_send()
+                total = held[pl.ds(base + z * n, n)].astype(F32) + single[...].astype(F32)
+                if last:
+                    self.put(total[0])
+                else:
+                    held[pl.ds(base + z * n, n)] = total.astype(LOW)
+
+        self.legs.append((begin_first, end_first))
+        self.legs.append((begin_second, end_second))
+
+    def step(self):
+        if self.at > 0:
+            self.legs[self.at - 1][1]()
+        if self.at < len(self.legs):
+            self.legs[self.at][0]()
+        self.at += 1
+
+
+class Gather:
+    def __init__(self, tiny):
+        self.steps = [tiny.gather_start] + [functools.partial(tiny.gather_step, i) for i in range(3)] + [tiny.gather_end]
+
+    def step(self):
+        self.steps.pop(0)()
+
+
+class Total:
+    def __init__(self, tiny, put):
+        self.steps = [tiny.sum_start] + [functools.partial(tiny.sum_step, i) for i in range(3)]
+        self.steps.append(lambda: put(tiny.sum_end()))
+
+    def step(self):
+        self.steps.pop(0)()
 
 
 def block_index(order, rest, z, y, x, c):
@@ -434,31 +503,61 @@
     return [(z, y, x, c) for z in range(rest) for y in range(2) for x in range(2) for c in range(2)]
 
 
-def staged_scratch(rest, order, rows, width):
-    sizes = {"x": 2, "y": 2, "z": rest}
-    blocks = 4 * rest
+def unit_scratch(order, rows, width):
+    blocks = 16
     bufs = [pltpu.VMEM((blocks, rows, width), LOW)]
     for axis in order:
-        blocks = blocks // sizes[axis]
-        copies = rest - 1 if axis == "z" else 1
-        bufs.append(pltpu.VMEM((copies * blocks, rows, width), LOW))
-    return bufs
-
-
-ORDERS = ("xyz", "yxz", "xyz", "yxz", "xzy", "yzx")
+        if axis == "z":
+            blocks = blocks // 4
+            bufs += [pltpu.VMEM((3 * blocks, rows, width), LOW), pltpu.VMEM((blocks, rows, width), LOW)]
+        else:
+            blocks = blocks // 2
+            bufs.append(pltpu.VMEM((blocks, rows, width), LOW))
+    return bufs + [pltpu.SemaphoreType.DMA((6,)), pltpu.SemaphoreType.DMA((6,))]
+
+
+ORDERS = ("xyz", "xyz", "zxy", "yzx", "yzx", "zxy", "xzy", "yxz", "xzy", "yxz", "xzy", "yxz")
+UNIT_PART = (0, 1, 2, 3, 0, 1, 2, 3, 0, 1, 2, 3)
+PLAN = (
+    (),
+    (),
+    (),
+    (),
+    (),
+    (0, 12),
+    (1, 2, 3),
+    (),
+    (),
+    (12,),
+    (),
+    (),
+    (),
+    (3, 4, 5, 6, 7, 0, 2, 12),
+    (1,),
+    (),
+    (8,),
+    (),
+    (3, 6, 2),
+    (),
+    (12,),
+    (3, 0, 2),
+    (8, 1, 5, 3),
+    (),
+    (9, 13, 10, 11, 2, 4, 7, 6, 0, 5, 1, 13, 7, 0, 6, 1, 5, 10, 8, 9, 6, 13, 4, 11, 5, 7, 8, 9, 10, 11, 8, 13, 7, 4, 9, 4, 11, 10, 9, 10, 11),
+)
 N_IN = 13
-N_OUT = 11
+N_OUT = 9
 
 
 def layer_kernel(rest, *refs):
     (lengths, labels, biases, gains, bias_up, w_class, tokens_h, cot_h, wqkv_h, wout_h, wup_h, wdown_h, wpool_h) = refs[:N_IN]
-    out_h, gtok_h, *sums = refs[N_IN : N_IN + 8]
-    small_out, everyone, loss_out = refs[N_IN + 8 : N_IN + N_OUT]
+    out_h, gtok_h, down_out, up_out, qkv_out, attn_out, small_out, everyone, loss_out = refs[N_IN : N_IN + N_OUT]
     scratch = list(refs[N_IN + N_OUT :])
     (
-        tokens, w_qkv, w_out, w_up, shared, packed, weights, inverse, context, normed_one, norm_low,
-        activated, slope, d_hidden, d_low, d_packed, part_down, scale_one, small, lead, in_sem, out_sem,
-    ) = scratch[:22]
+        tokens, w_qkv, w_out, w_up, w_down, packed, weights, inverse, context, normed_one, norm_low,
+        activated, slope, d_hidden, d_low, d_packed, part0, part1, part2, part3, scale_one, small, lead, in_sem, out_sem,
+    ) = scratch[:25]
+    parts = [part0, part1, part2, part3]
     cot = d_low
     d_context = norm_low
     wide = SLOT
@@ -467,8 +566,8 @@
     out_wide = d_packed.at[2 * D : 2 * D + SLOT]
     out_rest = d_packed.at[D : D + SLOT, wide // 2 : wide // 2 + D - wide]
     place = Place(rest)
-    small_bufs = scratch[22:32]
-    chunk_bufs = scratch[32:]
+    small_bufs = scratch[25:35]
+    unit_bufs = scratch[35:]
     head_rank = lax.axis_index("head")
     length = lengths[head_rank]
     label = labels[head_rank]
@@ -476,31 +575,48 @@
         pltpu.make_async_copy(src, dst, in_sem.at[i])
         for i, (src, dst) in enumerate(
             [(tokens_h, tokens), (wqkv_h, w_qkv), (wout_h, w_out), (wup_h, w_up),
-             (wdown_h, shared), (cot_h, cot), (wpool_h.at[:, 0:wide], pool_wide), (wpool_h.at[:, wide:D], pool_rest)]
+             (wdown_h, w_down), (cot_h, cot), (wpool_h.at[:, 0:wide], pool_wide), (wpool_h.at[:, wide:D], pool_rest)]
         )
     ]
-    for load in loads:
-        load.start()
+    loads[0].start()
+    loads[1].start()
     sem = pltpu.get_barrier_semaphore()
     for peer in (place.core_peer(), place.x_peer(), place.y_peer()):
         pl.semaphore_signal(sem, inc=1, device_id=peer, device_id_type=MESH)
     for offset in range(1, rest):
         pl.semaphore_signal(sem, inc=1, device_id=place.z_peer(offset), device_id_type=MESH)
 
-    half = FF // 2
-    per = 8 * rest
-    chunk_parts = [part_down.at[0:per], part_down.at[per : 2 * per]]
-    rows_up = FF // per // 2
-    shared_blocks = shared.reshape(2 * per, rows_up, D)
-    chunk_parts += [shared_blocks.at[0:per], shared_blocks.at[per : 2 * per]] * 2
-    chunks = []
-    for i in range(6):
-        own = chunk_bufs[8 * i : 8 * i + 8]
-        chunks.append(Staged(place, ORDERS[i], chunk_parts[i], own[:4], *own[4:]))
+    height = D // 32
+    order_of = owners(rest)
+
+    def put_down(i):
+        return lambda total: down_out.__setitem__((slice(None), slice(i * D, (i + 1) * D)), total)
+
+    def put_rows(ref, i):
+        return lambda total: ref.__setitem__(slice(i * height, (i + 1) * height), total)
+
     tiny = Small(place, small, lead, everyone, small_bufs)
+    puts = [put_down(i) for i in range(4)] + [put_rows(up_out, i) for i in range(4)] + [put_rows(attn_out, 0)]
+    puts += [put_rows(qkv_out, i) for i in range(3)]
+    units = []
+    at = 0
+    for i, order in enumerate(ORDERS):
+        size = len(unit_scratch(order, height, D))
+        own = unit_bufs[at : at + size]
+        at += size
+        units.append(Unit(place, order, parts[UNIT_PART[i]], own[:-2], own[-2], own[-1], puts[i]))
+    units.append(Gather(tiny))
+    units.append(Total(tiny, lambda total: small_out.__setitem__(Ellipsis, total)))
+    plan = list(PLAN)
+
+    def steps():
+        for i in plan.pop(0):
+            units[i].step()
 
     loads[0].wait()
     loads[1].wait()
+    for load in loads[2:]:
+        load.start()
     ones = jnp.ones((8, SLOT), LOW)
     for part in range(3):
         columns = slice(part * D, part * D + D)
@@ -558,7 +674,6 @@
 
     lax.fori_loop(0, FF // D, feed, 0)
 
-    w_down = shared
     for i in (4, 5, 6, 7):
         loads[i].wait()
     row = lax.broadcasted_iota(jnp.int32, (SLOT // 2, 1), 0)
@@ -625,163 +740,122 @@
     small[10:11] = gain_two
     small[7:8] = column_sum(ones, d_low[...])
 
+    rows = height
     for copy in out_copies:
         copy.wait()
     pl.semaphore_wait(sem, 3 + rest - 1)
-    tiny.gather_start()
+    units[12].step()
     d_branch_t = d_low[...].T
-    rows_down = D // per
-    for chunk in range(2):
-        for tile in range(4):
-            columns = slice(tile * D // 2, (tile + 1) * D // 2)
-            result = nn(d_branch_t, activated[:, chunk * half + columns.start : chunk * half + columns.stop])
-            for d, owner in enumerate(owners(rest)):
-                part_down[chunk * per + block_index(ORDERS[chunk], rest, *owner), :, columns] = (
-                    result[d * rows_down : (d + 1) * rows_down].astype(LOW)
-                )
-        chunks[chunk].start(0)
-
-    def feed_back(tile, carry):
-        columns = aligned(tile, D)
+    for i in range(4):
+        for columns in (slice(0, D // 2), slice(D // 2, D)):
+            result = nn(d_branch_t, activated[:, i * D + columns.start : i * D + columns.stop])
+            for d, owner in enumerate(order_of):
+                parts[i][block_index(ORDERS[i], rest, *owner), :, columns] = result[d * rows : (d + 1) * rows].astype(LOW)
+        units[i].step()
+        steps()
+
+    for tile in range(FF // D):
+        columns = slice(tile * D, (tile + 1) * D)
         d_up = (against(d_low[...], w_down[columns]) * slope[:, columns].astype(F32)).astype(LOW)
         slope[:, columns] = d_up
-        small[pl.ds(11 + tile, 1)] = column_sum(ones, d_up)
-        return carry
-
-    lax.fori_loop(0, FF // D, feed_back, 0)
+        small[11 + tile : 12 + tile] = column_sum(ones, d_up)
+        steps()
     d_up = slope
-    tiny.gather_step(0)
-    chunks[0].step(0)
-    chunks[1].step(0)
 
     for tile in range(FF // D):
         for columns in (slice(0, D // 2), slice(D // 2, D)):
             result = inner(d_up[:, tile * D : (tile + 1) * D], norm_low[:, columns])
-            for d in range(per * D // FF):
-                owner = owners(rest)[tile * (per * D // FF) + d]
-                for chunk in (2, 3):
-                    first = d * 2 * rows_up + (chunk - 2) * rows_up
-                    shared_blocks[(chunk - 2) * per + block_index(ORDERS[chunk], rest, *owner), :, columns] = (
-                        result[first : first + rows_up].astype(LOW)
-                    )
-    chunks[2].start(0)
-    chunks[3].start(0)
-    tiny.gather_step(1)
+            for d in range(8):
+                owner = order_of[tile * 8 + d]
+                for i in range(4):
+                    first = (d * 4 + i) * rows
+                    parts[i][block_index(ORDERS[4 + i], rest, *owner), :, columns] = result[first : first + rows].astype(LOW)
+        if tile == 3:
+            for i in range(4, 8):
+                units[i].step()
+        steps()
 
     shift_one = jnp.zeros((1, D), F32)
     gain_one = jnp.zeros((1, D), F32)
-    for rows in blocks:
-        d_norm = d_hidden[rows] + against(d_up[rows], w_up[...])
-        normed = normed_one[rows]
+    for block in blocks:
+        d_norm = d_hidden[block] + against(d_up[block], w_up[...])
+        normed = normed_one[block]
         shift_one = shift_one + jnp.sum(d_norm, axis=0, keepdims=True)
         gain_one = gain_one + jnp.sum(d_norm * normed, axis=0, keepdims=True)
-        d_one = normalized_back(normed, scale_one[rows], d_norm * gains[0:1])
-        d_hidden[rows] = d_one
-        d_low[rows] = d_one.astype(LOW)
+        d_one = normalized_back(normed, scale_one[block], d_norm * gains[0:1])
+        d_hidden[block] = d_one
+        d_low[block] = d_one.astype(LOW)
+        steps()
     small[6:7] = shift_one
     small[9:10] = gain_one
     small[5:6] = column_sum(ones, d_low[...])
-    chunks[2].step(0)
-    chunks[3].step(0)
-    tiny.gather_step(2)
-
+
+    result = inner(d_low[...], context[...])
+    for d, owner in enumerate(order_of):
+        parts[UNIT_PART[8]][block_index(ORDERS[8], rest, *owner)] = result[d * rows : (d + 1) * rows].astype(LOW)
+    units[8].step()
     d_context[...] = against(d_low[...], w_out[...]).astype(LOW)
-    result_out = inner(d_low[...], context[...])
-    own_qkv = 3 * D // per
-    own_out = D // per
-    first_rows = rows_up - (own_qkv - rows_up)
-    for d, owner in enumerate(owners(rest)):
-        shared_blocks[per + block_index(ORDERS[5], rest, *owner), own_qkv - rows_up :] = (
-            result_out[d * own_out : (d + 1) * own_out].astype(LOW)
-        )
-
-    def attend_back(pair, carry):
-        at = pl.multiple_of(pair * 2 * HEAD_DIM, 2 * HEAD_DIM)
-        queries_t = packed[:, pl.ds(at, 2 * HEAD_DIM)].T
-        keys_t = packed[:, pl.ds(at + D, 2 * HEAD_DIM)].T
-        values = packed[:, pl.ds(at + 2 * D, 2 * HEAD_DIM)]
-        context_t = context[:, pl.ds(at, 2 * HEAD_DIM)].T
-        d_context_t = d_context[:, pl.ds(at, 2 * HEAD_DIM)].T
+    steps()
+
+    def attend_back(pair):
+        at = pair * 2 * HEAD_DIM
+        queries_t = packed[:, at : at + 2 * HEAD_DIM].T
+        keys_t = packed[:, at + D : at + D + 2 * HEAD_DIM].T
+        values = packed[:, at + 2 * D : at + 2 * D + 2 * HEAD_DIM]
+        context_t = context[:, at : at + 2 * HEAD_DIM].T
+        d_context_t = d_context[:, at : at + 2 * HEAD_DIM].T
         scaled = []
         dots = []
         for k in range(2):
-            rows = slice(k * HEAD_DIM, (k + 1) * HEAD_DIM)
-            own = d_context_t[rows].astype(F32) * inverse[pair, k : k + 1]
-            dots.append(jnp.sum(own * context_t[rows].astype(F32), axis=0, keepdims=True))
+            own_rows = slice(k * HEAD_DIM, (k + 1) * HEAD_DIM)
+            own = d_context_t[own_rows].astype(F32) * inverse[pair, k : k + 1]
+            dots.append(jnp.sum(own * context_t[own_rows].astype(F32), axis=0, keepdims=True))
             scaled.append(own.astype(LOW))
         both = jnp.concatenate(scaled, axis=0).T
         for k in range(2):
-            rows = slice(k * HEAD_DIM, (k + 1) * HEAD_DIM)
+            own_rows = slice(k * HEAD_DIM, (k + 1) * HEAD_DIM)
             own_values = jnp.where(lane_of[k], values, jnp.zeros_like(values))
             powers = weights[2 * pair + k]
             d_scores = (powers.astype(F32) * (against(own_values, both) - dots[k])).astype(LOW)
-            put = pl.multiple_of(at + k * HEAD_DIM, HEAD_DIM)
-            d_packed[pl.ds(put, HEAD_DIM)] = (nn(keys_t[rows], d_scores) * HEAD_DIM ** (-0.5)).astype(LOW)
-            d_packed[pl.ds(put + D, HEAD_DIM)] = against(queries_t[rows], d_scores).astype(LOW)
-            d_packed[pl.ds(put + 2 * D, HEAD_DIM)] = against(scaled[k], powers).astype(LOW)
-        return carry
-
-    lax.fori_loop(0, 3, attend_back, 0)
-    chunks[0].step(1)
-    chunks[1].step(1)
-    lax.fori_loop(3, HEADS // 2, attend_back, 0)
-
-    for tile in range(rest):
-        size = 8 * own_qkv
-        result = nn(d_packed[tile * size : (tile + 1) * size], tokens[...])
-        for d in range(8):
-            owner = owners(rest)[tile * 8 + d]
-            first = d * own_qkv
-            shared_blocks[block_index(ORDERS[4], rest, *owner)] = result[first : first + rows_up].astype(LOW)
-            shared_blocks[per + block_index(ORDERS[5], rest, *owner), : own_qkv - rows_up] = (
-                result[first + rows_up : first + own_qkv].astype(LOW)
-            )
-    chunks[4].start(0)
-    chunks[5].start(0)
+            put = at + k * HEAD_DIM
+            d_packed[put : put + HEAD_DIM] = (nn(keys_t[own_rows], d_scores) * HEAD_DIM ** (-0.5)).astype(LOW)
+            d_packed[put + D : put + D + HEAD_DIM] = against(queries_t[own_rows], d_scores).astype(LOW)
+            d_packed[put + 2 * D : put + 2 * D + HEAD_DIM] = against(scaled[k], powers).astype(LOW)
+
+    for pair in range(HEADS // 2):
+        attend_back(pair)
+        steps()
+
     small[3:4] = against(ones, d_packed[0:D])[0:1]
     small[4:5] = against(ones, d_packed[2 * D : 3 * D])[0:1]
-    tiny.sum_start()
-    chunks[0].step(2)
-    chunks[1].step(2)
-
-    chunks[4].step(0)
-    chunks[5].step(0)
-    for k, rows in enumerate(blocks):
-        d_tokens = nn(w_qkv[...], d_packed[:, rows]).T + d_hidden[rows]
-        d_low[rows] = d_tokens.astype(LOW)
+    units[13].step()
+    for tile in range(rest):
+        result = nn(d_packed[tile * 24 * rows : (tile + 1) * 24 * rows], tokens[...])
+        for d in range(8):
+            owner = order_of[tile * 8 + d]
+            for i in range(3):
+                first = (d * 3 + i) * rows
+                parts[UNIT_PART[9 + i]][block_index(ORDERS[9 + i], rest, *owner)] = result[first : first + rows].astype(LOW)
+    for i in range(9, 12):
+        units[i].step()
+    steps()
+
+    for block in blocks:
+        d_tokens = nn(w_qkv[...], d_packed[:, block]).T + d_hidden[block]
+        d_low[block] = d_tokens.astype(LOW)
+        steps()
     token_copy = pltpu.make_async_copy(d_low, gtok_h, out_sem.at[1])
     token_copy.start()
-    tiny.sum_step(0)
-    chunks[2].step(1)
-    chunks[3].step(1)
-    sums[0][...] = chunks[0].finish()
-    sums[1][...] = chunks[1].finish()
-    tiny.sum_step(1)
-    chunks[2].step(2)
-    chunks[3].step(2)
-    tiny.sum_step(2)
-    chunks[4].step(1)
-    chunks[5].step(1)
-    sums[2][...] = chunks[2].finish()
-    sums[3][...] = chunks[3].finish()
-    small_out[...] = tiny.sum_end()
-    tiny.gather_end()
-    chunks[4].step(2)
-    chunks[5].step(2)
-    sums[4][...] = chunks[4].finish()
-    sums[5][...] = chunks[5].finish()
+    steps()
     token_copy.wait()
 
 
 def layer(rest, tokens, cotangent, lengths, labels, w_qkv, w_out, w_up, w_down, w_pool, w_class, biases, norm_gains, bias_up):
-    per = 8 * rest
-    rows_up = FF // per // 2
-    rows_down = D // per
+    rows = D // 32
     vmem = pl.BlockSpec(memory_space=pltpu.VMEM)
     smem = pl.BlockSpec(memory_space=pltpu.SMEM)
     anywhere = pl.BlockSpec(memory_space=pl.ANY)
     dma = pltpu.SemaphoreType.DMA
-    shapes = [(rows_down, FF // 2)] * 2 + [(rows_up, D)] * 4
     scratch = [
         pltpu.VMEM((SLOT, D), LOW),
         pltpu.VMEM((D, 3 * D), LOW),
@@ -799,16 +873,20 @@
         pltpu.VMEM((SLOT, D), F32),
         pltpu.VMEM((SLOT, D), LOW),
         pltpu.VMEM((3 * D, SLOT), LOW),
-        pltpu.VMEM((2 * per, rows_down, FF // 2), LOW),
+    ] + [pltpu.VMEM((32, rows, D), LOW)] * 4 + [
         pltpu.VMEM((SLOT, 1), F32),
         pltpu.VMEM((16, D), F32),
         pltpu.VMEM((2, D), F32),
         dma((8,)),
         dma((3,)),
     ] + small_scratch(rest)
-    for order, (rows, width) in zip(ORDERS, shapes):
-        scratch += staged_scratch(rest, order, rows, width) + [dma((4,)), dma((4,)), dma((rest - 1,)), dma((rest - 1,))]
-    outs = [jax.ShapeDtypeStruct((SLOT, D), LOW)] * 2 + [jax.ShapeDtypeStruct(shape, F32) for shape in shapes] + [
+    for order in ORDERS:
+        scratch += unit_scratch(order, rows, D)
+    outs = [jax.ShapeDtypeStruct((SLOT, D), LOW)] * 2 + [
+        jax.ShapeDtypeStruct((rows, FF), F32),
+        jax.ShapeDtypeStruct((4 * rows, D), F32),
+        jax.ShapeDtypeStruct((3 * rows, D), F32),
+        jax.ShapeDtypeStruct((rows, D), F32),
         jax.ShapeDtypeStruct((16, D), F32),
         jax.ShapeDtypeStruct((rest, 2, 2, 2, 2, D), F32),
         jax.ShapeDtypeStruct((1, 128), F32),
@@ -817,7 +895,7 @@
         functools.partial(layer_kernel, rest),
         out_shape=tuple(outs),
         in_specs=[smem, smem] + [vmem] * 4 + [anywhere] * 7,
-        out_specs=tuple([anywhere] * 2 + [vmem] * 9),
+        out_specs=tuple([anywhere] * 2 + [vmem] * 7),
         scratch_shapes=scratch,
         compiler_params=pltpu.CompilerParams(
             collective_id=0, has_side_effects=True, vmem_limit_bytes=61 << 20
@@ -826,25 +904,21 @@
 
 
 def finish_kernel(rest, *refs):
-    out_in, gtok_in, down1, down2, up1, up2, last1, last2, small, everyone, loss = refs[:11]
-    (out, gtok, losses, g_qkv, g_out, g_up, g_down, g_pool, g_class, g_biases, g_gains, g_bias_up, g_pool_bias) = refs[11:24]
-    sem = refs[24]
-    copies = [pltpu.make_async_copy(out_in, out, sem.at[0]), pltpu.make_async_copy(gtok_in, gtok, sem.at[1])]
-    for copy in copies:
+    *moved, small, everyone, loss = refs[:9]
+    targets = refs[9:15]
+    losses, g_pool, g_class, g_biases, g_gains, g_bias_up, g_pool_bias = refs[15:22]
+    *stages, sem_in, sem_out = refs[22:]
+    arrive = [pltpu.make_async_copy(src, mid, sem_in.at[i]) for i, (src, mid) in enumerate(zip(moved, stages))]
+    leave = [pltpu.make_async_copy(mid, dst, sem_out.at[i]) for i, (mid, dst) in enumerate(zip(stages, targets))]
+    for copy in arrive:
         copy.start()
-    per = 8 * rest
+    for before, after in zip(arrive, leave):
+        before.wait()
+        after.start()
     rank = lax.axis_index("batch") * 4 + lax.axis_index("head")
-    own = D // per
-    own_qkv = 3 * own
-    own_up = FF // per
-    rows_up = own_up // 2
+    own = D // (8 * rest)
+    own_up = 4 * own
     losses[...] = loss[0:1, 0:1]
-    g_down[0 : FF // 2] = down1[...].T
-    g_down[FF // 2 : FF] = down2[...].T
-    g_up[...] = jnp.concatenate([up1[...], up2[...]], axis=0).T
-    last = jnp.concatenate([last1[...], last2[...]], axis=0).T
-    g_qkv[...] = last[:, :own_qkv]
-    g_out[...] = last[:, own_qkv:]
 
     def window(array, start, size):
         at = lax.broadcasted_iota(jnp.int32, (D, size), 0)
@@ -858,42 +932,40 @@
     g_pool_bias[...] = picked[15:16]
     flat = rank * own_up
     part = flat // D
-    rows = small[11:15]
     pick = lax.broadcasted_iota(jnp.int32, (4, 1), 0) == part
-    chosen = jnp.sum(jnp.where(pick, rows, 0.0), axis=0, keepdims=True)
+    chosen = jnp.sum(jnp.where(pick, small[11:15], 0.0), axis=0, keepdims=True)
     g_bias_up[...] = window(jnp.broadcast_to(chosen, (8, D)), flat - part * D, own_up)[0:1]
-    leading = everyone[:, 0]
     d_pre = window(everyone[:, 1], rank * own, own)
     g_pool[...] = lax.dot_general(
-        leading, d_pre, (((0,), (0,)), ((), ())), precision=lax.Precision.HIGHEST, preferred_element_type=F32
+        d_pre, everyone[:, 0], (((0,), (0,)), ((), ())), precision=lax.Precision.HIGHEST, preferred_element_type=F32
     )
-    for copy in copies:
+    for copy in leave:
         copy.wait()
 
 
 def finish(rest, results):
-    per = 8 * rest
-    own = D // per
+    own = D // (8 * rest)
     vmem = pl.BlockSpec(memory_space=pltpu.VMEM)
     anywhere = pl.BlockSpec(memory_space=pl.ANY)
     shape = lambda *s: jax.ShapeDtypeStruct(s, F32)
     results = list(results)
-    results[9] = results[9].reshape(per, 2, D)
+    results[7] = results[7].reshape(8 * rest, 2, D)
     outs = [jax.ShapeDtypeStruct((SLOT, D), LOW)] * 2 + [
-        shape(1, 1), shape(D, 3 * own), shape(D, own), shape(D, 4 * own), shape(FF, own), shape(D, own),
-        shape(3, own), shape(6, own), shape(2, own), shape(1, 4 * own), shape(1, own),
+        shape(own, FF), shape(4 * own, D), shape(3 * own, D), shape(own, D),
+        shape(1, 1), shape(own, D), shape(3, own), shape(6, own), shape(2, own), shape(1, 4 * own), shape(1, own),
     ]
-    out = list(pl.pallas_call(
+    (out, gtok, down, up, qkv, attn, losses, pool, g_class, g_biases, g_gains, g_bias_up, g_pool_bias) = pl.pallas_call(
         functools.partial(finish_kernel, rest),
         out_shape=tuple(outs),
-        in_specs=[anywhere] * 2 + [vmem] * 9,
-        out_specs=tuple([anywhere] * 2 + [vmem] * 11),
-        scratch_shapes=[pltpu.SemaphoreType.DMA((2,))],
-        compiler_params=pltpu.CompilerParams(vmem_limit_bytes=32 << 20),
-    )(*results))
-    for i in (2, 11, 12):
-        out[i] = out[i].reshape(-1)
-    return tuple(out)
+        in_specs=[anywhere] * 6 + [vmem] * 3,
+        out_specs=tuple([anywhere] * 6 + [vmem] * 7),
+        scratch_shapes=[pltpu.VMEM(o.shape, o.dtype) for o in outs[:6]] + [pltpu.SemaphoreType.DMA((6,))] * 2,
+        compiler_params=pltpu.CompilerParams(vmem_limit_bytes=60 << 20),
+    )(*results)
+    return (
+        out, gtok, losses.reshape(-1), qkv.T, attn.T, up.T, down.T, pool.T, g_class, g_biases, g_gains,
+        g_bias_up.reshape(-1), g_pool_bias.reshape(-1),
+    )
 
 
 def per_device(
@@ -912,7 +984,7 @@
     bias_up,
 ):
     rest = lax.axis_size("batch") // 2
-    if D // (8 * rest) % 8 == 0:
+    if rest == 4:
         return finish(rest, layer(
             rest, tokens, cotangent, lengths, labels, w_qkv, w_out, w_up, w_down, w_pool, w_class, biases, norm_gains,
             bias_up,

time: 154 us -> 116 us (0.75)
  Pallas kernels: 138 us -> 115 us
  local copies, waits for them, and re-layouts: 14.5 us -> 0 us
    pallas_call x1, Pallas kernels: 136 us -> 111 us  [layer(): pl.pallas_call(functools.partial(layer_kernel, rest), out_shape=tuple(out...]
    unnamed x27 -> x0, local copies, waits for them, and re-layouts: 14.5 us -> none
    pallas_call x1, Pallas kernels: 2.2 us -> 4.23 us  [finish(): pl.pallas_call(functools.partial(finish_kernel, rest), out_shape=tuple(ou...]
where the time goes in v1:
time: 116 us
  Pallas kernels  115 us (99%)
    pallas_call x1, Pallas kernels, layer(): pl.pallas_call(functools.partial(layer_kernel, rest), out_shape=tuple(out...  111 us
    pallas_call x1, Pallas kernels, finish(): pl.pallas_call(functools.partial(finish_kernel, rest), out_shape=tuple(ou...  4.23 us

profile of v1, /device:TPU:0, one launch (start us, length us, event | category | flops | bytes accessed | tf_op | source)
XLA Modules:
  0.0 115.9 jit_solution(9869906346511276776)
XLA Ops:
  0.6 110.8 %shard_map.228 = (bf16[512,768]{1,0:T(8,128)(2,1)}, bf16[512,768]{1,0:T(8,128)(2,1)}, f32[24,3072]{1,0:T(8,128)}, f32[96,768]{1,0:T(8,128)}, f32[72,768]{1,0:T(8...) custom-call(s32[4]{0:T(128)} %refs_0_.1, s32[4]{0:T(128)} %refs_1_.1, ...), custom_call_target="tpu_custom_call" | custom-call | tf_op jit(solution)/shard_map/pallas_call | solution.py:894
  111.5 4.2 %shard_map.229 = (bf16[512,768]{1,0:T(8,128)(2,1)}, bf16[512,768]{1,0:T(8,128)(2,1)}, f32[24,3072]{1,0:T(8,128)}, f32[96,768]{1,0:T(8,128)}, f32[72,768]{1,0:T(8...) custom-call(bf16[512,768]{1,0:T(8,128)(2,1)} %get-tuple-element.35.r, ...), custom_call_target="tpu_custom_call" | custom-call | tf_op jit(solution)/shard_map/pallas_call | solution.py:957

commit v2 on v1

--- a/solution.py
+++ b/solution.py
@@ -389,6 +389,11 @@
             copy.wait()
             if last:
                 self.put(got[0].astype(F32) + own[start].astype(F32))
+            elif count >= 8:
+                def add(i, carry):
+                    got[pl.ds(i * 4, 4)] = got[pl.ds(i * 4, 4)] + own[pl.ds(start + i * 4, 4)]
+                    return carry
+                lax.fori_loop(0, count // 4, add, 0)
             else:
                 got[...] = got[...] + own[pl.ds(start, count)]
         return end
@@ -474,20 +479,54 @@
 
 
 class Gather:
-    def __init__(self, tiny):
-        self.steps = [tiny.gather_start] + [functools.partial(tiny.gather_step, i) for i in range(3)] + [tiny.gather_end]
+    def __init__(self, place, lead, everyone, send, recv):
+        p = place
+        peers = (p.core_peer(), p.x_peer(), p.y_peer())
+        own = everyone.at[p.z, p.y, p.x, p.c]
+        blocks = (own, everyone.at[p.z, p.y, p.x], everyone.at[p.z, p.y])
+        groups = [[remote(blocks[i], blocks[i], send.at[i], recv.at[i], peers[i])] for i in range(3)]
+        groups.append([
+            remote(everyone.at[p.z], everyone.at[p.z], send.at[k + 2], recv.at[k + 2], p.z_peer(k)) for k in range(1, p.rest)
+        ])
+        self.groups, self.at, self.own, self.lead = groups, 0, own, lead
 
     def step(self):
-        self.steps.pop(0)()
+        if self.at == 0:
+            self.own[...] = self.lead[...]
+        else:
+            for copy in self.groups[self.at - 1]:
+                copy.wait()
+        if self.at < 4:
+            for copy in self.groups[self.at]:
+                copy.start()
+        self.at += 1
 
 
 class Total:
-    def __init__(self, tiny, put):
-        self.steps = [tiny.sum_start] + [functools.partial(tiny.sum_step, i) for i in range(3)]
-        self.steps.append(lambda: put(tiny.sum_end()))
+    def __init__(self, place, small, low, got, send, recv, put):
+        p = place
+        peers = (p.core_peer(), p.x_peer(), p.y_peer())
+        groups = [[remote(low, got.at[i], send.at[i], recv.at[i], peers[i])] for i in range(3)]
+        groups.append([
+            remote(low, got.at[k + 2], send.at[k + 2], recv.at[k + 2], p.z_peer(k)) for k in range(1, p.rest)
+        ])
+        self.groups, self.at, self.small, self.low, self.got, self.put = groups, 0, small, low, got, put
 
     def step(self):
-        self.steps.pop(0)()
+        total = self.small[...]
+        if self.at > 0:
+            first = self.at - 1
+            for i, copy in enumerate(self.groups[first]):
+                copy.wait()
+                total = total + self.got[first + i].astype(F32)
+        if self.at < 4:
+            self.small[...] = total
+            self.low[...] = total.astype(LOW)
+            for copy in self.groups[self.at]:
+                copy.start()
+        else:
+            self.put(total)
+        self.at += 1
 
 
 def block_index(order, rest, z, y, x, c):
@@ -516,34 +555,33 @@
     return bufs + [pltpu.SemaphoreType.DMA((6,)), pltpu.SemaphoreType.DMA((6,))]
 
 
-ORDERS = ("xyz", "xyz", "zxy", "yzx", "yzx", "zxy", "xzy", "yxz", "xzy", "yxz", "xzy", "yxz")
-UNIT_PART = (0, 1, 2, 3, 0, 1, 2, 3, 0, 1, 2, 3)
+UNITS = (("down", 4, 2), ("up", 4, 1), ("out", 1, 1), ("qkv", 3, 2))
+ORDERS = (
+    "zyx", "yzx", "xyz", "yxz", "yzx", "xzy", "zyx", "yzx", "xyz", "zyx", "yxz", "yxz", "xyz", "yxz", "xyz", "yxz", "xzy", "yxz", "xzy",
+)
 PLAN = (
     (),
     (),
     (),
     (),
     (),
-    (0, 12),
-    (1, 2, 3),
+    (19,),
+    (0,),
+    (1,),
+    (3, 7, 6, 19, 5,),
+    (1, 4, 2,),
+    (5,),
+    (3, 7, 6, 2, 19, 0, 8,),
+    (1, 10, 9,),
+    (2,),
+    (12, 11, 3,),
+    (8, 10,),
     (),
+    (5, 4,),
+    (11, 12, 9, 10, 6, 5,),
+    (20, 8, 15, 16, 12, 18, 7, 3, 13, 11, 2, 5, 20, 8, 17, 14, 16,),
     (),
-    (12,),
-    (),
-    (),
-    (),
-    (3, 4, 5, 6, 7, 0, 2, 12),
-    (1,),
-    (),
-    (8,),
-    (),
-    (3, 6, 2),
-    (),
-    (12,),
-    (3, 0, 2),
-    (8, 1, 5, 3),
-    (),
-    (9, 13, 10, 11, 2, 4, 7, 6, 0, 5, 1, 13, 7, 0, 6, 1, 5, 10, 8, 9, 6, 13, 4, 11, 5, 7, 8, 9, 10, 11, 8, 13, 7, 4, 9, 4, 11, 10, 9, 10, 11),
+    (10, 0, 18, 11, 15, 13, 3, 6, 20, 4, 14, 16, 17, 15, 9, 7, 18, 13, 14, 12, 0, 20, 4, 16, 17, 1, 7, 11, 6, 15, 19, 9, 2, 13, 18, 14, 10, 16, 12, 4, 1, 17, 9, 0, 8, 13, 15, 18, 14, 17,),
 )
 N_IN = 13
 N_OUT = 9
@@ -566,20 +604,21 @@
     out_wide = d_packed.at[2 * D : 2 * D + SLOT]
     out_rest = d_packed.at[D : D + SLOT, wide // 2 : wide // 2 + D - wide]
     place = Place(rest)
-    small_bufs = scratch[25:35]
-    unit_bufs = scratch[35:]
+    small_bufs = scratch[25:31]
+    unit_bufs = scratch[31:]
     head_rank = lax.axis_index("head")
     length = lengths[head_rank]
     label = labels[head_rank]
     loads = [
         pltpu.make_async_copy(src, dst, in_sem.at[i])
         for i, (src, dst) in enumerate(
-            [(tokens_h, tokens), (wqkv_h, w_qkv), (wout_h, w_out), (wup_h, w_up),
+            [(tokens_h, tokens), (wqkv_h.at[:, 0:D], w_qkv.at[:, 0:D]), (wqkv_h.at[:, D : 2 * D], w_qkv.at[:, D : 2 * D]),
+             (wqkv_h.at[:, 2 * D :], w_qkv.at[:, 2 * D :]), (wout_h, w_out), (wup_h, w_up),
              (wdown_h, w_down), (cot_h, cot), (wpool_h.at[:, 0:wide], pool_wide), (wpool_h.at[:, wide:D], pool_rest)]
         )
     ]
-    loads[0].start()
-    loads[1].start()
+    for load in loads[:4]:
+        load.start()
     sem = pltpu.get_barrier_semaphore()
     for peer in (place.core_peer(), place.x_peer(), place.y_peer()):
         pl.semaphore_signal(sem, inc=1, device_id=peer, device_id_type=MESH)
@@ -589,24 +628,51 @@
     height = D // 32
     order_of = owners(rest)
 
-    def put_down(i):
-        return lambda total: down_out.__setitem__((slice(None), slice(i * D, (i + 1) * D)), total)
-
-    def put_rows(ref, i):
-        return lambda total: ref.__setitem__(slice(i * height, (i + 1) * height), total)
-
-    tiny = Small(place, small, lead, everyone, small_bufs)
-    puts = [put_down(i) for i in range(4)] + [put_rows(up_out, i) for i in range(4)] + [put_rows(attn_out, 0)]
-    puts += [put_rows(qkv_out, i) for i in range(3)]
+    targets = {"down": down_out, "up": up_out, "out": attn_out, "qkv": qkv_out}
+    base_part = {"down": 0, "up": 0, "out": 0, "qkv": 1}
+
+    def put_into(kind, i, columns):
+        def put(total):
+            if kind == "down":
+                down_out[:, i * D + columns.start : i * D + columns.stop] = total
+            else:
+                targets[kind][i * height : (i + 1) * height, columns] = total
+        return put
+
     units = []
+    number = {}
     at = 0
-    for i, order in enumerate(ORDERS):
-        size = len(unit_scratch(order, height, D))
-        own = unit_bufs[at : at + size]
-        at += size
-        units.append(Unit(place, order, parts[UNIT_PART[i]], own[:-2], own[-2], own[-1], puts[i]))
-    units.append(Gather(tiny))
-    units.append(Total(tiny, lambda total: small_out.__setitem__(Ellipsis, total)))
+    for kind, count, cut in UNITS:
+        for i in range(count):
+            for j in range(cut):
+                columns = slice(j * D // cut, (j + 1) * D // cut)
+                order = ORDERS[len(units)]
+                size = len(unit_scratch(order, height, D // cut))
+                own = unit_bufs[at : at + size]
+                at += size
+                part = parts[base_part[kind] + i]
+                if cut > 1:
+                    part = part.at[:, :, columns]
+                number[kind, i, j] = len(units)
+                units.append(Unit(place, order, part, own[:-2], own[-2], own[-1], put_into(kind, i, columns)))
+    gather, totals = len(units), len(units) + 1
+
+    def fill(kind, i, owner, columns, value):
+        cut = {name: c for name, _, c in UNITS}[kind]
+        width = D // cut
+        part = parts[base_part[kind] + i]
+        for j in range(cut):
+            first, last = max(columns.start, j * width), min(columns.stop, (j + 1) * width)
+            if first < last:
+                index = block_index(ORDERS[number[kind, i, j]], rest, *owner)
+                part[index, :, first:last] = value[:, first - columns.start : last - columns.start].astype(LOW)
+
+    def go(kind, i, j):
+        units[number[kind, i, j]].step()
+
+    low_small, got_small, *small_sems = small_bufs
+    units.append(Gather(place, lead, everyone, *small_sems[:2]))
+    units.append(Total(place, small, low_small, got_small, *small_sems[2:], lambda total: small_out.__setitem__(Ellipsis, total)))
     plan = list(PLAN)
 
     def steps():
@@ -614,12 +680,13 @@
             units[i].step()
 
     loads[0].wait()
-    loads[1].wait()
-    for load in loads[2:]:
-        load.start()
     ones = jnp.ones((8, SLOT), LOW)
     for part in range(3):
         columns = slice(part * D, part * D + D)
+        loads[part + 1].wait()
+        if part == 0:
+            for load in loads[4:]:
+                load.start()
         result = nn(tokens[...], w_qkv[:, columns])
         if part == 0:
             result = (result + biases[0:1]).astype(LOW) * jnp.asarray(HEAD_DIM ** (-0.5), LOW)
@@ -633,11 +700,11 @@
     lane = lax.broadcasted_iota(jnp.int32, (1, 2 * HEAD_DIM), 1)
     lane_of = [lane < HEAD_DIM, lane >= HEAD_DIM]
 
-    def attend(pair, carry):
-        at = pl.multiple_of(pair * 2 * HEAD_DIM, 2 * HEAD_DIM)
-        queries = packed[:, pl.ds(at, 2 * HEAD_DIM)]
-        keys_all = packed[:, pl.ds(at + D, 2 * HEAD_DIM)]
-        values_t = packed[:, pl.ds(at + 2 * D, 2 * HEAD_DIM)].T
+    def attend(pair):
+        at = pair * 2 * HEAD_DIM
+        queries = packed[:, at : at + 2 * HEAD_DIM]
+        keys_all = packed[:, at + D : at + D + 2 * HEAD_DIM]
+        values_t = packed[:, at + 2 * D : at + 2 * D + 2 * HEAD_DIM].T
         got = []
         for k in range(2):
             own_keys = jnp.where(lane_of[k], keys_all, jnp.zeros_like(keys_all))
@@ -648,13 +715,13 @@
             weights[2 * pair + k] = powers
             inverse[pair, k : k + 1] = inv
             got.append(nn(values_t[k * HEAD_DIM : (k + 1) * HEAD_DIM], powers) * inv)
-        context[:, pl.ds(at, 2 * HEAD_DIM)] = jnp.concatenate(got, axis=0).T.astype(LOW)
-        return carry
-
-    lax.fori_loop(0, HEADS // 2, attend, 0)
+        context[:, at : at + 2 * HEAD_DIM] = jnp.concatenate(got, axis=0).T.astype(LOW)
+
+    for pair in range(HEADS // 2):
+        attend(pair)
 
     blocks = [slice(0, SLOT // 2), slice(SLOT // 2, SLOT)]
-    loads[2].wait()
+    loads[4].wait()
     for rows in blocks:
         hidden = nn(context[rows], w_out[...]) + biases[2:3] + tokens[rows].astype(F32)
         normed, scale = normalized(hidden)
@@ -662,19 +729,19 @@
         scale_one[rows] = scale
         norm_low[rows] = (normed * gains[0:1] + biases[3:4]).astype(LOW)
 
-    loads[3].wait()
-
-    def feed(tile, carry):
-        columns = aligned(tile, D)
+    loads[5].wait()
+
+    def feed(tile):
+        columns = slice(tile * D, (tile + 1) * D)
         hidden = nn(norm_low[...], w_up[:, columns]) + bias_up[0:1, columns]
         share = 0.5 + 0.5 * lax.erf(hidden * 0.7071067811865476)
         activated[:, columns] = (hidden * share).astype(LOW)
         slope[:, columns] = (share + hidden * (jnp.exp(-0.5 * hidden * hidden) * 0.3989422804014327)).astype(LOW)
-        return carry
-
-    lax.fori_loop(0, FF // D, feed, 0)
-
-    for i in (4, 5, 6, 7):
+
+    for tile in range(FF // D):
+        feed(tile)
+
+    for i in (6, 7, 8, 9):
         loads[i].wait()
     row = lax.broadcasted_iota(jnp.int32, (SLOT // 2, 1), 0)
     kept = []
@@ -720,8 +787,8 @@
     d_leading = jnp.sum(d_leading, axis=0, keepdims=True)
     small[0:3] = d_logits * pooled_low
     small[15:16] = d_pre
-    lead[0:1] = leading[0:1].astype(F32)
-    lead[1:2] = d_pre
+    lead[0:1] = leading[0:1]
+    lead[1:2] = d_pre.astype(LOW)
 
     shift_two = jnp.zeros((1, D), F32)
     gain_two = jnp.zeros((1, D), F32)
@@ -744,36 +811,48 @@
     for copy in out_copies:
         copy.wait()
     pl.semaphore_wait(sem, 3 + rest - 1)
-    units[12].step()
+    units[gather].step()
     d_branch_t = d_low[...].T
+    halves = (slice(0, D // 2), slice(D // 2, D))
+    everything = slice(0, D)
+    cuts = {name: cut for name, _, cut in UNITS}
     for i in range(4):
-        for columns in (slice(0, D // 2), slice(D // 2, D)):
+        for j, columns in enumerate(halves):
             result = nn(d_branch_t, activated[:, i * D + columns.start : i * D + columns.stop])
             for d, owner in enumerate(order_of):
-                parts[i][block_index(ORDERS[i], rest, *owner), :, columns] = result[d * rows : (d + 1) * rows].astype(LOW)
-        units[i].step()
-        steps()
-
-    for tile in range(FF // D):
-        columns = slice(tile * D, (tile + 1) * D)
+                fill("down", i, owner, columns, result[d * rows : (d + 1) * rows])
+            if cuts["down"] == 2:
+                go("down", i, j)
+            elif j == 1:
+                go("down", i, 0)
+            steps()
+
+    def feed_back(tile, carry):
+        columns = aligned(tile, D)
         d_up = (against(d_low[...], w_down[columns]) * slope[:, columns].astype(F32)).astype(LOW)
         slope[:, columns] = d_up
-        small[11 + tile : 12 + tile] = column_sum(ones, d_up)
+        small[pl.ds(11 + tile, 1)] = column_sum(ones, d_up)
+        return carry
+
+    for part in range(2):
+        lax.fori_loop(2 * part, 2 * part + 2, feed_back, 0)
         steps()
     d_up = slope
 
-    for tile in range(FF // D):
-        for columns in (slice(0, D // 2), slice(D // 2, D)):
-            result = inner(d_up[:, tile * D : (tile + 1) * D], norm_low[:, columns])
+    def up_gradient(tile, carry):
+        for columns in halves:
+            result = inner(d_up[:, aligned(tile, D)], norm_low[:, columns])
             for d in range(8):
-                owner = order_of[tile * 8 + d]
                 for i in range(4):
                     first = (d * 4 + i) * rows
-                    parts[i][block_index(ORDERS[4 + i], rest, *owner), :, columns] = result[first : first + rows].astype(LOW)
-        if tile == 3:
-            for i in range(4, 8):
-                units[i].step()
-        steps()
+                    fill("up", i, (tile, *order_of[d][1:]), columns, result[first : first + rows])
+        return carry
+
+    lax.fori_loop(0, FF // D, up_gradient, 0)
+    for i in range(4):
+        for j in range(cuts["up"]):
+            go("up", i, j)
+    steps()
 
     shift_one = jnp.zeros((1, D), F32)
     gain_one = jnp.zeros((1, D), F32)
@@ -792,18 +871,19 @@
 
     result = inner(d_low[...], context[...])
     for d, owner in enumerate(order_of):
-        parts[UNIT_PART[8]][block_index(ORDERS[8], rest, *owner)] = result[d * rows : (d + 1) * rows].astype(LOW)
-    units[8].step()
+        fill("out", 0, owner, everything, result[d * rows : (d + 1) * rows])
+    for j in range(cuts["out"]):
+        go("out", 0, j)
     d_context[...] = against(d_low[...], w_out[...]).astype(LOW)
     steps()
 
-    def attend_back(pair):
-        at = pair * 2 * HEAD_DIM
-        queries_t = packed[:, at : at + 2 * HEAD_DIM].T
-        keys_t = packed[:, at + D : at + D + 2 * HEAD_DIM].T
-        values = packed[:, at + 2 * D : at + 2 * D + 2 * HEAD_DIM]
-        context_t = context[:, at : at + 2 * HEAD_DIM].T
-        d_context_t = d_context[:, at : at + 2 * HEAD_DIM].T
+    def attend_back(pair, carry):
+        at = pl.multiple_of(pair * 2 * HEAD_DIM, 2 * HEAD_DIM)
+        queries_t = packed[:, pl.ds(at, 2 * HEAD_DIM)].T
+        keys_t = packed[:, pl.ds(at + D, 2 * HEAD_DIM)].T
+        values = packed[:, pl.ds(at + 2 * D, 2 * HEAD_DIM)]
+        context_t = context[:, pl.ds(at, 2 * HEAD_DIM)].T
+        d_context_t = d_context[:, pl.ds(at, 2 * HEAD_DIM)].T
         scaled = []
         dots = []
         for k in range(2):
@@ -817,27 +897,32 @@
             own_values = jnp.where(lane_of[k], values, jnp.zeros_like(values))
             powers = weights[2 * pair + k]
             d_scores = (powers.astype(F32) * (against(own_values, both) - dots[k])).astype(LOW)
-            put = at + k * HEAD_DIM
-            d_packed[put : put + HEAD_DIM] = (nn(keys_t[own_rows], d_scores) * HEAD_DIM ** (-0.5)).astype(LOW)
-            d_packed[put + D : put + D + HEAD_DIM] = against(queries_t[own_rows], d_scores).astype(LOW)
-            d_packed[put + 2 * D : put + 2 * D + HEAD_DIM] = against(scaled[k], powers).astype(LOW)
-
-    for pair in range(HEADS // 2):
-        attend_back(pair)
+            put = pl.multiple_of(at + k * HEAD_DIM, HEAD_DIM)
+            d_packed[pl.ds(put, HEAD_DIM)] = (nn(keys_t[own_rows], d_scores) * HEAD_DIM ** (-0.5)).astype(LOW)
+            d_packed[pl.ds(put + D, HEAD_DIM)] = against(queries_t[own_rows], d_scores).astype(LOW)
+            d_packed[pl.ds(put + 2 * D, HEAD_DIM)] = against(scaled[k], powers).astype(LOW)
+        return carry
+
+    for part in range(3):
+        lax.fori_loop(2 * part, 2 * part + 2, attend_back, 0)
         steps()
 
     small[3:4] = against(ones, d_packed[0:D])[0:1]
     small[4:5] = against(ones, d_packed[2 * D : 3 * D])[0:1]
-    units[13].step()
-    for tile in range(rest):
-        result = nn(d_packed[tile * 24 * rows : (tile + 1) * 24 * rows], tokens[...])
+    units[totals].step()
+    steps()
+    def qkv_gradient(tile, carry):
+        result = nn(d_packed[aligned(tile, 24 * rows)], tokens[...])
         for d in range(8):
-            owner = order_of[tile * 8 + d]
             for i in range(3):
                 first = (d * 3 + i) * rows
-                parts[UNIT_PART[9 + i]][block_index(ORDERS[9 + i], rest, *owner)] = result[first : first + rows].astype(LOW)
-    for i in range(9, 12):
-        units[i].step()
+                fill("qkv", i, (tile, *order_of[d][1:]), everything, result[first : first + rows])
+        return carry
+
+    lax.fori_loop(0, rest, qkv_gradient, 0)
+    for i in range(3):
+        for j in range(cuts["qkv"]):
+            go("qkv", i, j)
     steps()
 
     for block in blocks:
@@ -876,19 +961,27 @@
     ] + [pltpu.VMEM((32, rows, D), LOW)] * 4 + [
         pltpu.VMEM((SLOT, 1), F32),
         pltpu.VMEM((16, D), F32),
-        pltpu.VMEM((2, D), F32),
-        dma((8,)),
+        pltpu.VMEM((2, D), LOW),
+        dma((10,)),
         dma((3,)),
-    ] + small_scratch(rest)
-    for order in ORDERS:
-        scratch += unit_scratch(order, rows, D)
+        pltpu.VMEM((16, D), LOW),
+        pltpu.VMEM((6, 16, D), LOW),
+        dma((6,)),
+        dma((6,)),
+        dma((6,)),
+        dma((6,)),
+    ]
+    orders = list(ORDERS)
+    for _, count, cut in UNITS:
+        for _ in range(count * cut):
+            scratch += unit_scratch(orders.pop(0), rows, D // cut)
     outs = [jax.ShapeDtypeStruct((SLOT, D), LOW)] * 2 + [
         jax.ShapeDtypeStruct((rows, FF), F32),
         jax.ShapeDtypeStruct((4 * rows, D), F32),
         jax.ShapeDtypeStruct((3 * rows, D), F32),
         jax.ShapeDtypeStruct((rows, D), F32),
         jax.ShapeDtypeStruct((16, D), F32),
-        jax.ShapeDtypeStruct((rest, 2, 2, 2, 2, D), F32),
+        jax.ShapeDtypeStruct((rest, 2, 2, 2, 2, D), LOW),
         jax.ShapeDtypeStruct((1, 128), F32),
     ]
     return pl.pallas_call(
@@ -935,9 +1028,9 @@
     pick = lax.broadcasted_iota(jnp.int32, (4, 1), 0) == part
     chosen = jnp.sum(jnp.where(pick, small[11:15], 0.0), axis=0, keepdims=True)
     g_bias_up[...] = window(jnp.broadcast_to(chosen, (8, D)), flat - part * D, own_up)[0:1]
-    d_pre = window(everyone[:, 1], rank * own, own)
+    d_pre = window(everyone[:, 1].astype(F32), rank * own, own)
     g_pool[...] = lax.dot_general(
-        d_pre, everyone[:, 0], (((0,), (0,)), ((), ())), precision=lax.Precision.HIGHEST, preferred_element_type=F32
+        d_pre, everyone[:, 0].astype(F32), (((0,), (0,)), ((), ())), precision=lax.Precision.HIGHEST, preferred_element_type=F32
     )
     for copy in leave:
         copy.wait()

time: 116 us -> 97.3 us (0.84)
  Pallas kernels: 115 us -> 96.2 us
    pallas_call x1, Pallas kernels: 111 us -> 92 us  [layer(): pl.pallas_call(functools.partial(layer_kernel, rest), out_shape=tuple(out...]
where the time goes in v2:
time: 97.3 us; the launch traced here: 97.1 us
  Pallas kernels  96.2 us (99%)
    pallas_call x1, Pallas kernels, layer(): pl.pallas_call(functools.partial(layer_kernel, rest), out_shape=tuple(out...  92 us
    pallas_call x1, Pallas kernels, finish(): pl.pallas_call(functools.partial(finish_kernel, rest), out_shape=tuple(ou...  4.19 us

profile of v2, /device:TPU:0, one launch (start us, length us, event | category | flops | bytes accessed | tf_op | source)
XLA Modules:
  0.0 97.1 jit_solution(6143667406927917014)
XLA Ops:
  0.6 92.0 %shard_map.228 = (bf16[512,768]{1,0:T(8,128)(2,1)}, bf16[512,768]{1,0:T(8,128)(2,1)}, f32[24,3072]{1,0:T(8,128)}, f32[96,768]{1,0:T(8,128)}, f32[72,768]{1,0:T(8...) custom-call(s32[4]{0:T(128)} %refs_0_.1, s32[4]{0:T(128)} %refs_1_.1, ...), custom_call_target="tpu_custom_call" | custom-call | tf_op jit(solution)/shard_map/pallas_call | solution.py:987
  92.7 4.2 %shard_map.229 = (bf16[512,768]{1,0:T(8,128)(2,1)}, bf16[512,768]{1,0:T(8,128)(2,1)}, f32[24,3072]{1,0:T(8,128)}, f32[96,768]{1,0:T(8,128)}, f32[72,768]{1,0:T(8...) custom-call(bf16[512,768]{1,0:T(8,128)(2,1)} %get-tuple-element.35.r, ...), custom_call_target="tpu_custom_call" | custom-call | tf_op jit(solution)/shard_map/pallas_call | solution.py:1050

commit v3 on v2

--- a/solution.py
+++ b/solution.py
@@ -338,10 +338,6 @@
     return pl.ds(pl.multiple_of(index * step, step), step)
 
 
-def column_sum(ones, array):
-    return nn(ones, array)[0:1]
-
-
 def normalized(hidden):
     center = hidden - jnp.mean(hidden, axis=-1, keepdims=True)
     spread = jnp.mean(center * center, axis=-1, keepdims=True)
@@ -356,9 +352,9 @@
 
 
 class Unit:
-    def __init__(self, place, order, part, bufs, send, recv, put):
+    def __init__(self, place, order, part, bufs, send, recv, put, after):
         p = self.place = place
-        self.put = put
+        self.put, self.after = put, after
         self.at = 0
         self.legs = []
         bufs = list(bufs)
@@ -475,11 +471,14 @@
             self.legs[self.at - 1][1]()
         if self.at < len(self.legs):
             self.legs[self.at][0]()
+        else:
+            self.after()
         self.at += 1
 
 
 class Gather:
-    def __init__(self, place, lead, everyone, send, recv):
+    def __init__(self, place, lead, everyone, send, recv, after):
+        self.after = after
         p = place
         peers = (p.core_peer(), p.x_peer(), p.y_peer())
         own = everyone.at[p.z, p.y, p.x, p.c]
@@ -499,6 +498,8 @@
         if self.at < 4:
             for copy in self.groups[self.at]:
                 copy.start()
+        else:
+            self.after()
         self.at += 1
 
 
@@ -555,9 +556,9 @@
     return bufs + [pltpu.SemaphoreType.DMA((6,)), pltpu.SemaphoreType.DMA((6,))]
 
 
-UNITS = (("down", 4, 2), ("up", 4, 1), ("out", 1, 1), ("qkv", 3, 2))
+UNITS = (("down", 4, 1), ("up", 4, 1), ("out", 1, 1), ("qkv", 3, 3))
 ORDERS = (
-    "zyx", "yzx", "xyz", "yxz", "yzx", "xzy", "zyx", "yzx", "xyz", "zyx", "yxz", "yxz", "xyz", "yxz", "xyz", "yxz", "xzy", "yxz", "xzy",
+    "xyz", "zxy", "yzx", "xzy", "zxy", "yxz", "xyz", "yxz", "xyz", "yzx", "yxz", "xyz", "xyz", "xyz", "xyz", "yxz", "yxz", "yxz",
 )
 PLAN = (
     (),
@@ -565,31 +566,31 @@
     (),
     (),
     (),
-    (19,),
-    (0,),
-    (1,),
-    (3, 7, 6, 19, 5,),
-    (1, 4, 2,),
-    (5,),
-    (3, 7, 6, 2, 19, 0, 8,),
-    (1, 10, 9,),
-    (2,),
-    (12, 11, 3,),
-    (8, 10,),
     (),
-    (5, 4,),
-    (11, 12, 9, 10, 6, 5,),
-    (20, 8, 15, 16, 12, 18, 7, 3, 13, 11, 2, 5, 20, 8, 17, 14, 16,),
     (),
-    (10, 0, 18, 11, 15, 13, 3, 6, 20, 4, 14, 16, 17, 15, 9, 7, 18, 13, 14, 12, 0, 20, 4, 16, 17, 1, 7, 11, 6, 15, 19, 9, 2, 13, 18, 14, 10, 16, 12, 4, 1, 17, 9, 0, 8, 13, 15, 18, 14, 17,),
+    (),
+    (1, 0, 2,),
+    (3,),
+    (),
+    (0, 2,),
+    (5, 4, 1, 6,),
+    (7,),
+    (8,),
+    (),
+    (3,),
+    (5, 2, 6,),
+    (8, 0, 7, 4, 9, 6, 18, 11,),
+    (5, 10, 14, 0, 8, 12, 17, 3, 13, 6, 18, 9, 16, 7, 14, 15, 10,),
+    (),
+    (8, 17, 0, 18, 12, 11, 16, 9, 19, 4, 13, 10, 5, 14, 17, 15, 7, 1, 16, 12, 19, 2, 9, 11, 3, 8, 10, 13, 6, 17, 15, 4, 14, 16, 7, 19, 12, 1, 11, 5, 13, 9, 3, 15, 10, 18, 14, 17, 16, 2, 12, 4, 11, 1, 13, 19, 15,),
 )
 N_IN = 13
 N_OUT = 9
 
 
 def layer_kernel(rest, *refs):
-    (lengths, labels, biases, gains, bias_up, w_class, tokens_h, cot_h, wqkv_h, wout_h, wup_h, wdown_h, wpool_h) = refs[:N_IN]
-    out_h, gtok_h, down_out, up_out, qkv_out, attn_out, small_out, everyone, loss_out = refs[N_IN : N_IN + N_OUT]
+    (lengths, labels, biases_h, gains_h, bias_up_h, w_class_h, tokens_h, cot_h, wqkv_h, wout_h, wup_h, wdown_h, wpool_h) = refs[:N_IN]
+    out_h, gtok_h, down_out, up_out, qkv_out, attn_out, small_out, everyone_out, loss_out = refs[N_IN : N_IN + N_OUT]
     scratch = list(refs[N_IN + N_OUT :])
     (
         tokens, w_qkv, w_out, w_up, w_down, packed, weights, inverse, context, normed_one, norm_low,
@@ -605,7 +606,14 @@
     out_rest = d_packed.at[D : D + SLOT, wide // 2 : wide // 2 + D - wide]
     place = Place(rest)
     small_bufs = scratch[25:31]
-    unit_bufs = scratch[31:]
+    biases, gains, bias_up, w_class = scratch[31:35]
+    down_mid, up_mid, qkv_mid, attn_mid, small_mid, everyone, loss_mid = scratch[35:42]
+    little_sem, done_sem = scratch[42:44]
+    unit_bufs = scratch[44:]
+    little = [
+        pltpu.make_async_copy(src, dst, little_sem.at[i])
+        for i, (src, dst) in enumerate([(biases_h, biases), (gains_h, gains), (bias_up_h, bias_up), (w_class_h, w_class)])
+    ]
     head_rank = lax.axis_index("head")
     length = lengths[head_rank]
     label = labels[head_rank]
@@ -617,7 +625,7 @@
              (wdown_h, w_down), (cot_h, cot), (wpool_h.at[:, 0:wide], pool_wide), (wpool_h.at[:, wide:D], pool_rest)]
         )
     ]
-    for load in loads[:4]:
+    for load in loads[:4] + little:
         load.start()
     sem = pltpu.get_barrier_semaphore()
     for peer in (place.core_peer(), place.x_peer(), place.y_peer()):
@@ -628,16 +636,26 @@
     height = D // 32
     order_of = owners(rest)
 
-    targets = {"down": down_out, "up": up_out, "out": attn_out, "qkv": qkv_out}
+    targets = {"down": (down_mid, down_out), "up": (up_mid, up_out), "out": (attn_mid, attn_out), "qkv": (qkv_mid, qkv_out)}
+    leaving = []
+
+    def leave(src, dst, i):
+        copy = pltpu.make_async_copy(src, dst, done_sem.at[i])
+        copy.start()
+        leaving.append(copy)
     base_part = {"down": 0, "up": 0, "out": 0, "qkv": 1}
 
-    def put_into(kind, i, columns):
+    def put_into(kind, i, columns, n):
+        if kind == "down":
+            place_of = (slice(None), slice(i * D + columns.start, i * D + columns.stop))
+        else:
+            place_of = (slice(i * height, (i + 1) * height), columns)
+        mid, out = targets[kind]
+
         def put(total):
-            if kind == "down":
-                down_out[:, i * D + columns.start : i * D + columns.stop] = total
-            else:
-                targets[kind][i * height : (i + 1) * height, columns] = total
-        return put
+            mid[place_of] = total
+
+        return put, lambda: leave(mid.at[place_of], out.at[place_of], n)
 
     units = []
     number = {}
@@ -654,9 +672,8 @@
                 if cut > 1:
                     part = part.at[:, :, columns]
                 number[kind, i, j] = len(units)
-                units.append(Unit(place, order, part, own[:-2], own[-2], own[-1], put_into(kind, i, columns)))
-    gather, totals = len(units), len(units) + 1
-
+                put, after = put_into(kind, i, columns, len(units))
+                units.append(Unit(place, order, part, own[:-2], own[-2], own[-1], put, after))
     def fill(kind, i, owner, columns, value):
         cut = {name: c for name, _, c in UNITS}[kind]
         width = D // cut
@@ -671,8 +688,14 @@
         units[number[kind, i, j]].step()
 
     low_small, got_small, *small_sems = small_bufs
-    units.append(Gather(place, lead, everyone, *small_sems[:2]))
-    units.append(Total(place, small, low_small, got_small, *small_sems[2:], lambda total: small_out.__setitem__(Ellipsis, total)))
+    gather, totals = len(units), len(units) + 1
+
+    def put_small(total):
+        small_mid[...] = total
+        leave(small_mid, small_out, totals)
+
+    units.append(Gather(place, lead, everyone, *small_sems[:2], lambda: leave(everyone, everyone_out, gather)))
+    units.append(Total(place, small, low_small, got_small, *small_sems[2:], put_small))
     plan = list(PLAN)
 
     def steps():
@@ -680,6 +703,8 @@
             units[i].step()
 
     loads[0].wait()
+    for load in little:
+        load.wait()
     ones = jnp.ones((8, SLOT), LOW)
     for part in range(3):
         columns = slice(part * D, part * D + D)
@@ -699,6 +724,8 @@
     key_live = lax.broadcasted_iota(jnp.int32, (SLOT, 1), 0) < length
     lane = lax.broadcasted_iota(jnp.int32, (1, 2 * HEAD_DIM), 1)
     lane_of = [lane < HEAD_DIM, lane >= HEAD_DIM]
+    spare = [lane == HEAD_DIM, lane == 0]
+    dead = [jnp.where(jnp.logical_and(spare[k], jnp.logical_not(key_live)), -1e30, 0.0).astype(LOW) for k in range(2)]
 
     def attend(pair):
         at = pair * 2 * HEAD_DIM
@@ -707,8 +734,8 @@
         values_t = packed[:, at + 2 * D : at + 2 * D + 2 * HEAD_DIM].T
         got = []
         for k in range(2):
-            own_keys = jnp.where(lane_of[k], keys_all, jnp.zeros_like(keys_all))
-            scores = jnp.where(key_live, against(own_keys, queries), -1e30)
+            own_keys = jnp.where(lane_of[k], keys_all, dead[k])
+            scores = against(own_keys, jnp.where(lane_of[k], queries, jnp.ones_like(queries)))
             powers = jnp.exp(scores - jnp.max(scores, axis=0, keepdims=True))
             inv = 1.0 / jnp.sum(powers, axis=0, keepdims=True)
             powers = powers.astype(LOW)
@@ -772,9 +799,10 @@
     powers = jnp.exp(logits - top)
     total = jnp.sum(powers, axis=0, keepdims=True)
     onehot = (lax.broadcasted_iota(jnp.int32, (CLASSES, 1), 0) == label).astype(F32)
-    loss_out[...] = jnp.broadcast_to(
-        jnp.log(total) + top - jnp.sum(onehot * logits, axis=0, keepdims=True), loss_out.shape
+    loss_mid[...] = jnp.broadcast_to(
+        jnp.log(total) + top - jnp.sum(onehot * logits, axis=0, keepdims=True), loss_mid.shape
     )
+    leave(loss_mid, loss_out, totals + 1)
     d_logits = powers / total - onehot
     d_pre = jnp.sum(d_logits * classes, axis=0, keepdims=True) * (1.0 - pooled * pooled)
     high = d_pre.astype(LOW).astype(F32)
@@ -792,6 +820,7 @@
 
     shift_two = jnp.zeros((1, D), F32)
     gain_two = jnp.zeros((1, D), F32)
+    bias_down = jnp.zeros((1, D), F32)
     for k in (1, 0):
         rows = blocks[k]
         normed, scale = d_hidden[rows], kept[k]
@@ -802,10 +831,12 @@
         gain_two = gain_two + jnp.sum(d_out * normed, axis=0, keepdims=True)
         d_two = normalized_back(normed, scale, d_out * gains[1:2])
         d_hidden[rows] = d_two
-        d_low[rows] = d_two.astype(LOW)
+        d_two = d_two.astype(LOW)
+        d_low[rows] = d_two
+        bias_down = bias_down + jnp.sum(d_two.astype(F32), axis=0, keepdims=True)
     small[8:9] = shift_two
     small[10:11] = gain_two
-    small[7:8] = column_sum(ones, d_low[...])
+    small[7:8] = bias_down
 
     rows = height
     for copy in out_copies:
@@ -827,16 +858,13 @@
                 go("down", i, 0)
             steps()
 
-    def feed_back(tile, carry):
-        columns = aligned(tile, D)
+    for tile in range(FF // D):
+        columns = slice(tile * D, (tile + 1) * D)
         d_up = (against(d_low[...], w_down[columns]) * slope[:, columns].astype(F32)).astype(LOW)
         slope[:, columns] = d_up
-        small[pl.ds(11 + tile, 1)] = column_sum(ones, d_up)
-        return carry
-
-    for part in range(2):
-        lax.fori_loop(2 * part, 2 * part + 2, feed_back, 0)
-        steps()
+        small[11 + tile : 12 + tile] = jnp.sum(d_up.astype(F32), axis=0, keepdims=True)
+        if tile % 2 == 1:
+            steps()
     d_up = slope
 
     def up_gradient(tile, carry):
@@ -856,6 +884,7 @@
 
     shift_one = jnp.zeros((1, D), F32)
     gain_one = jnp.zeros((1, D), F32)
+    bias_attn = jnp.zeros((1, D), F32)
     for block in blocks:
         d_norm = d_hidden[block] + against(d_up[block], w_up[...])
         normed = normed_one[block]
@@ -863,11 +892,13 @@
         gain_one = gain_one + jnp.sum(d_norm * normed, axis=0, keepdims=True)
         d_one = normalized_back(normed, scale_one[block], d_norm * gains[0:1])
         d_hidden[block] = d_one
-        d_low[block] = d_one.astype(LOW)
+        d_one = d_one.astype(LOW)
+        d_low[block] = d_one
+        bias_attn = bias_attn + jnp.sum(d_one.astype(F32), axis=0, keepdims=True)
         steps()
     small[6:7] = shift_one
     small[9:10] = gain_one
-    small[5:6] = column_sum(ones, d_low[...])
+    small[5:6] = bias_attn
 
     result = inner(d_low[...], context[...])
     for d, owner in enumerate(order_of):
@@ -933,6 +964,8 @@
     token_copy.start()
     steps()
     token_copy.wait()
+    for copy in leaving:
+        copy.wait()
 
 
 def layer(rest, tokens, cotangent, lengths, labels, w_qkv, w_out, w_up, w_down, w_pool, w_class, biases, norm_gains, bias_up):
@@ -970,11 +1003,11 @@
         dma((6,)),
         dma((6,)),
         dma((6,)),
+        pltpu.VMEM(biases.shape, F32),
+        pltpu.VMEM(norm_gains.shape, F32),
+        pltpu.VMEM((1, FF), F32),
+        pltpu.VMEM(w_class.shape, LOW),
     ]
-    orders = list(ORDERS)
-    for _, count, cut in UNITS:
-        for _ in range(count * cut):
-            scratch += unit_scratch(orders.pop(0), rows, D // cut)
     outs = [jax.ShapeDtypeStruct((SLOT, D), LOW)] * 2 + [
         jax.ShapeDtypeStruct((rows, FF), F32),
         jax.ShapeDtypeStruct((4 * rows, D), F32),
@@ -984,11 +1017,17 @@
         jax.ShapeDtypeStruct((rest, 2, 2, 2, 2, D), LOW),
         jax.ShapeDtypeStruct((1, 128), F32),
     ]
+    scratch += [pltpu.VMEM(o.shape, o.dtype) for o in outs[2:]]
+    scratch += [dma((4,)), dma((len(ORDERS) + 3,))]
+    orders = list(ORDERS)
+    for _, count, cut in UNITS:
+        for _ in range(count * cut):
+            scratch += unit_scratch(orders.pop(0), rows, D // cut)
     return pl.pallas_call(
         functools.partial(layer_kernel, rest),
         out_shape=tuple(outs),
-        in_specs=[smem, smem] + [vmem] * 4 + [anywhere] * 7,
-        out_specs=tuple([anywhere] * 2 + [vmem] * 7),
+        in_specs=[smem, smem] + [anywhere] * 11,
+        out_specs=tuple([anywhere] * 9),
         scratch_shapes=scratch,
         compiler_params=pltpu.CompilerParams(
             collective_id=0, has_side_effects=True, vmem_limit_bytes=61 << 20
@@ -997,20 +1036,21 @@
 
 
 def finish_kernel(rest, *refs):
-    *moved, small, everyone, loss = refs[:9]
-    targets = refs[9:15]
-    losses, g_pool, g_class, g_biases, g_gains, g_bias_up, g_pool_bias = refs[15:22]
-    *stages, sem_in, sem_out = refs[22:]
-    arrive = [pltpu.make_async_copy(src, mid, sem_in.at[i]) for i, (src, mid) in enumerate(zip(moved, stages))]
-    leave = [pltpu.make_async_copy(mid, dst, sem_out.at[i]) for i, (mid, dst) in enumerate(zip(stages, targets))]
+    moved, tables = refs[:6], refs[6:9]
+    targets, rest_out = refs[9:15], refs[15:22]
+    stages, tables_in, results = refs[22:28], refs[28:31], refs[31:38]
+    sem_in, sem_out = refs[38:]
+    arrive = [pltpu.make_async_copy(src, mid, sem_in.at[i]) for i, (src, mid) in enumerate(zip(tables + moved, tables_in + stages))]
+    leave = [pltpu.make_async_copy(mid, dst, sem_out.at[i]) for i, (mid, dst) in enumerate(zip(stages + results, targets + rest_out))]
     for copy in arrive:
         copy.start()
-    for before, after in zip(arrive, leave):
-        before.wait()
-        after.start()
+    small, everyone, loss = tables_in
+    losses, g_pool, g_class, g_biases, g_gains, g_bias_up, g_pool_bias = results
     rank = lax.axis_index("batch") * 4 + lax.axis_index("head")
     own = D // (8 * rest)
     own_up = 4 * own
+    for copy in arrive[:3]:
+        copy.wait()
     losses[...] = loss[0:1, 0:1]
 
     def window(array, start, size):
@@ -1018,7 +1058,10 @@
         want = lax.broadcasted_iota(jnp.int32, (D, size), 1)
         return exact(array, (at == want + start).astype(F32))
 
-    picked = window(small[...], rank * own, own)
+    leading = everyone[:, 0].astype(F32)
+    d_pre = everyone[:, 1].astype(F32)
+    both = window(jnp.concatenate([small[...], d_pre], axis=0), rank * own, own)
+    picked = both[0:16]
     g_class[...] = picked[0:3]
     g_biases[...] = picked[3:9]
     g_gains[...] = picked[9:11]
@@ -1028,17 +1071,20 @@
     pick = lax.broadcasted_iota(jnp.int32, (4, 1), 0) == part
     chosen = jnp.sum(jnp.where(pick, small[11:15], 0.0), axis=0, keepdims=True)
     g_bias_up[...] = window(jnp.broadcast_to(chosen, (8, D)), flat - part * D, own_up)[0:1]
-    d_pre = window(everyone[:, 1].astype(F32), rank * own, own)
     g_pool[...] = lax.dot_general(
-        d_pre, everyone[:, 0].astype(F32), (((0,), (0,)), ((), ())), precision=lax.Precision.HIGHEST, preferred_element_type=F32
+        both[16:], leading, (((0,), (0,)), ((), ())), precision=lax.Precision.HIGHEST, preferred_element_type=F32
     )
+    for before, after in zip(arrive[3:], leave):
+        before.wait()
+        after.start()
+    for copy in leave[6:]:
+        copy.start()
     for copy in leave:
         copy.wait()
 
 
 def finish(rest, results):
     own = D // (8 * rest)
-    vmem = pl.BlockSpec(memory_space=pltpu.VMEM)
     anywhere = pl.BlockSpec(memory_space=pl.ANY)
     shape = lambda *s: jax.ShapeDtypeStruct(s, F32)
     results = list(results)
@@ -1047,12 +1093,14 @@
         shape(own, FF), shape(4 * own, D), shape(3 * own, D), shape(own, D),
         shape(1, 1), shape(own, D), shape(3, own), shape(6, own), shape(2, own), shape(1, 4 * own), shape(1, own),
     ]
+    held = lambda arrays: [pltpu.VMEM(o.shape, o.dtype) for o in arrays]
     (out, gtok, down, up, qkv, attn, losses, pool, g_class, g_biases, g_gains, g_bias_up, g_pool_bias) = pl.pallas_call(
         functools.partial(finish_kernel, rest),
         out_shape=tuple(outs),
-        in_specs=[anywhere] * 6 + [vmem] * 3,
-        out_specs=tuple([anywhere] * 6 + [vmem] * 7),
-        scratch_shapes=[pltpu.VMEM(o.shape, o.dtype) for o in outs[:6]] + [pltpu.SemaphoreType.DMA((6,))] * 2,
+        in_specs=[anywhere] * 9,
+        out_specs=tuple([anywhere] * 13),
+        scratch_shapes=held(outs[:6]) + held(results[6:]) + held(outs[6:])
+        + [pltpu.SemaphoreType.DMA((9,)), pltpu.SemaphoreType.DMA((13,))],
         compiler_params=pltpu.CompilerParams(vmem_limit_bytes=60 << 20),
     )(*results)
     return (

time: 97.3 us -> 94.6 us (0.972)
  Pallas kernels: 96.2 us -> 93.6 us
    pallas_call x1, Pallas kernels: 92 us -> 90.3 us  [layer(): pl.pallas_call(functools.partial(layer_kernel, rest), out_shape=tuple(out...]
where the time goes in v3:
time: 94.6 us; the launch traced here: 94.4 us
  Pallas kernels  93.6 us (99%)
    pallas_call x1, Pallas kernels, layer(): pl.pallas_call(functools.partial(layer_kernel, rest), out_shape=tuple(out...  90.3 us
    pallas_call x1, Pallas kernels, finish(): pl.pallas_call(functools.partial(finish_kernel, rest), out_shape=tuple(ou...  3.3 us

profile of v3, /device:TPU:0, one launch (start us, length us, event | category | flops | bytes accessed | tf_op | source)
XLA Modules:
  0.0 94.4 jit_solution(6825081379469702724)
XLA Ops:
  0.6 90.3 %shard_map.228 = (bf16[512,768]{1,0:T(8,128)(2,1)}, bf16[512,768]{1,0:T(8,128)(2,1)}, f32[24,3072]{1,0:T(8,128)}, f32[96,768]{1,0:T(8,128)}, f32[72,768]{1,0:T(8...) custom-call(s32[4]{0:T(128)} %refs_0_.1, s32[4]{0:T(128)} %refs_1_.1, ...), custom_call_target="tpu_custom_call" | custom-call | tf_op jit(solution)/shard_map/pallas_call | solution.py:1026
  90.9 3.3 %shard_map.229 = (bf16[512,768]{1,0:T(8,128)(2,1)}, bf16[512,768]{1,0:T(8,128)(2,1)}, f32[24,3072]{1,0:T(8,128)}, f32[96,768]{1,0:T(8,128)}, f32[72,768]{1,0:T(8...) custom-call(bf16[512,768]{1,0:T(8,128)(2,1)} %get-tuple-element.35.r, ...), custom_call_target="tpu_custom_call" | custom-call | tf_op jit(solution)/shard_map/pallas_call | solution.py:1097

commit v4 on v3

--- a/solution.py
+++ b/solution.py
@@ -558,7 +558,7 @@
 
 UNITS = (("down", 4, 1), ("up", 4, 1), ("out", 1, 1), ("qkv", 3, 3))
 ORDERS = (
-    "xyz", "zxy", "yzx", "xzy", "zxy", "yxz", "xyz", "yxz", "xyz", "yzx", "yxz", "xyz", "xyz", "xyz", "xyz", "yxz", "yxz", "yxz",
+    "zxy", "xyz", "yzx", "xyz", "yxz", "zyx", "xzy", "yxz", "xyz", "yxz", "xyz", "xzy", "yxz", "yxz", "yxz", "yxz", "xyz", "xyz",
 )
 PLAN = (
     (),
@@ -569,20 +569,20 @@
     (),
     (),
     (),
-    (1, 0, 2,),
+    (0, 1, 2,),
     (3,),
     (),
-    (0, 2,),
-    (5, 4, 1, 6,),
-    (7,),
-    (8,),
+    (1, 2,),
+    (4,),
+    (6, 5, 0,),
+    (7, 8,),
     (),
-    (3,),
-    (5, 2, 6,),
-    (8, 0, 7, 4, 9, 6, 18, 11,),
-    (5, 10, 14, 0, 8, 12, 17, 3, 13, 6, 18, 9, 16, 7, 14, 15, 10,),
+    (6,),
+    (4, 3, 2,),
+    (8, 1, 7, 5, 3, 18, 9, 11, 4, 14,),
+    (16, 17, 7, 10, 18, 15, 1, 6, 11, 13, 9, 14, 16, 8, 4, 12,),
     (),
-    (8, 17, 0, 18, 12, 11, 16, 9, 19, 4, 13, 10, 5, 14, 17, 15, 7, 1, 16, 12, 19, 2, 9, 11, 3, 8, 10, 13, 6, 17, 15, 4, 14, 16, 7, 19, 12, 1, 11, 5, 13, 9, 3, 15, 10, 18, 14, 17, 16, 2, 12, 4, 11, 1, 13, 19, 15,),
+    (15, 17, 18, 19, 11, 1, 3, 10, 16, 13, 5, 9, 7, 14, 6, 12, 8, 15, 0, 19, 17, 2, 13, 10, 9, 3, 11, 14, 5, 12, 18, 15, 16, 19, 17, 0, 13, 7, 11, 10, 2, 5, 12, 15, 8, 14, 9, 6, 16, 4, 17, 0, 13, 10, 19, 12,),
 )
 N_IN = 13
 N_OUT = 9
@@ -839,8 +839,6 @@
     small[7:8] = bias_down
 
     rows = height
-    for copy in out_copies:
-        copy.wait()
     pl.semaphore_wait(sem, 3 + rest - 1)
     units[gather].step()
     d_branch_t = d_low[...].T
@@ -934,6 +932,8 @@
             d_packed[pl.ds(put + 2 * D, HEAD_DIM)] = against(scaled[k], powers).astype(LOW)
         return carry
 
+    for copy in out_copies:
+        copy.wait()
     for part in range(3):
         lax.fori_loop(2 * part, 2 * part + 2, attend_back, 0)
         steps()
@@ -1049,6 +1049,9 @@
     rank = lax.axis_index("batch") * 4 + lax.axis_index("head")
     own = D // (8 * rest)
     own_up = 4 * own
+    for before, after in zip(arrive[3:], leave):
+        before.wait()
+        after.start()
     for copy in arrive[:3]:
         copy.wait()
     losses[...] = loss[0:1, 0:1]
@@ -1074,9 +1077,6 @@
     g_pool[...] = lax.dot_general(
         both[16:], leading, (((0,), (0,)), ((), ())), precision=lax.Precision.HIGHEST, preferred_element_type=F32
     )
-    for before, after in zip(arrive[3:], leave):
-        before.wait()
-        after.start()
     for copy in leave[6:]:
         copy.start()
     for copy in leave:

time: 94.6 us -> 94.3 us (level)
  no operation moved by 1% of the time
where the time goes in v4:
time: 94.3 us; the launch traced here: 94 us
  Pallas kernels  93.2 us (99%)
    pallas_call x1, Pallas kernels, layer(): pl.pallas_call(functools.partial(layer_kernel, rest), out_shape=tuple(out...  89.9 us
    pallas_call x1, Pallas kernels, finish(): pl.pallas_call(functools.partial(finish_kernel, rest), out_shape=tuple(ou...  3.26 us

profile of v4, /device:TPU:0, one launch (start us, length us, event | category | flops | bytes accessed | tf_op | source)
XLA Modules:
  0.0 94.0 jit_solution(12593855426960702477)
XLA Ops:
  0.6 89.9 %shard_map.228 = (bf16[512,768]{1,0:T(8,128)(2,1)}, bf16[512,768]{1,0:T(8,128)(2,1)}, f32[24,3072]{1,0:T(8,128)}, f32[96,768]{1,0:T(8,128)}, f32[72,768]{1,0:T(8...) custom-call(s32[4]{0:T(128)} %refs_0_.1, s32[4]{0:T(128)} %refs_1_.1, ...), custom_call_target="tpu_custom_call" | custom-call | tf_op jit(solution)/shard_map/pallas_call | solution.py:1026
  90.6 3.3 %shard_map.229 = (bf16[512,768]{1,0:T(8,128)(2,1)}, bf16[512,768]{1,0:T(8,128)(2,1)}, f32[24,3072]{1,0:T(8,128)}, f32[96,768]{1,0:T(8,128)}, f32[72,768]{1,0:T(8...) custom-call(bf16[512,768]{1,0:T(8,128)(2,1)} %get-tuple-element.35.r, ...), custom_call_target="tpu_custom_call" | custom-call | tf_op jit(solution)/shard_map/pallas_call | solution.py:1097
